TPU v7x, 768 devices: a whole 4x8x12 slice. The times are simulated.
768 devices in a mesh: band: 192 (over z, x_hi, y), group: 4 (over x_lo, core).
Axes of the slice: x: 4 (x_hi: 2, x_lo: 2; x = x_hi * 2 + x_lo), y: 8, z: 12, core: 2. Of those that a mesh axis runs over, the one named last changes fastest.
Arguments:
- trial: bfloat16 [192, 64, 4096], P('band'), may hold values from -6 to 6
- orbitals: bfloat16 [768, 64, 4096], P(('band', 'group')), may hold values from -6 to 6
- labels: int32 [768], P(('band', 'group')), may hold values from 0 to 767, each once
- kernel_mask: int32 [64, 4096], replicated, may hold values from 0 to 1, as said below
Outputs:
- exchange_field: float32 [192, 64, 4096], P('band', 'group')
Inputs may be any that keep to these rules, and one draw needn't show every extreme that they name: `labels`: a permutation of the source orbitals' numbers. `kernel_mask`: unchanged when any one frequency index k is replaced by (64 - k) mod 64.
All inputs are finite; a program needn't handle non-finite values.
Results may differ from a plain program's by a relative error of at most 0.009.
Values may be sent and summed in bfloat16 or wider, within the bound.
No kernel may reach another device: no remote copies, remote signals or barrier semaphores. Data moves between devices by JAX's collectives and lax.ppermute only.
A program may use at most 32 MiB of HBM per device.

v0:
```python
import jax
import jax.numpy as jnp
from jax import lax
from jax.sharding import PartitionSpec as P

WINDOW = 2


screen_square = 16.0


def passed_along(value, axis, steps):
    count = lax.axis_size(axis)
    pairs = [(source, (source + steps) % count) for source in range(count)]
    return lax.ppermute(value, axis, pairs)


def cas_table(grid_size):
    frequency = jnp.arange(grid_size, dtype=jnp.int32)
    product = frequency[:, None] * frequency[None, :] % grid_size
    phase_angle = product.astype(jnp.float32) * (2.0 * jnp.pi / grid_size)
    return (
        (jnp.cos(phase_angle) + jnp.sin(phase_angle)) / jnp.sqrt(jnp.float32(grid_size))
    ).astype(jnp.bfloat16)


def screened_kernel(mask_cube):
    grid_size = mask_cube.shape[0]
    frequency = jnp.arange(grid_size, dtype=jnp.int32)
    signed = jnp.where(frequency < grid_size // 2, frequency, frequency - grid_size)
    squared = signed * signed
    q_square = squared[:, None, None] + squared[None, :, None] + squared[None, None, :]
    return (
        mask_cube.astype(jnp.float32)
        * screen_square
        / (q_square.astype(jnp.float32) + screen_square)
    )


def occupation(label_values, orbital_count):
    shifted = (label_values.astype(jnp.float32) - orbital_count / 2.0) / (orbital_count / 4.0)
    return 1.0 / (1.0 + jnp.exp(shifted))


def axis_pass(field_data, hartley):
    return lax.dot_general(
        field_data, hartley, (((0,), (0,)), ((), ())), preferred_element_type=jnp.float32
    )


def pair_contribution(target, source_orbital, weight, hartley, kernel):
    density = (target.astype(jnp.float32) * source_orbital.astype(jnp.float32)).astype(jnp.bfloat16)
    first = axis_pass(density, hartley).astype(jnp.bfloat16)
    second = axis_pass(first, hartley).astype(jnp.bfloat16)
    spectrum = (axis_pass(second, hartley) * kernel).astype(jnp.bfloat16)
    back_first = axis_pass(spectrum, hartley).astype(jnp.bfloat16)
    back_second = axis_pass(back_first, hartley).astype(jnp.bfloat16)
    potential = axis_pass(back_second, hartley)
    return weight * potential * source_orbital.astype(jnp.float32)


def shards(trial, orbitals, labels, kernel_mask):
    grid_size = trial.shape[1]
    orbital_count = lax.axis_size("band") * lax.axis_size("group")
    hartley = cas_table(grid_size)
    kernel = screened_kernel(kernel_mask.reshape(grid_size, grid_size, grid_size))
    target = trial[0].reshape(grid_size, grid_size, grid_size)
    sources = []
    current, current_tags = (orbitals, labels)
    for offset in range(WINDOW):
        sources.append((current[0], current_tags[0]))
        if offset + 1 < WINDOW:
            current, current_tags = passed_along((current, current_tags), "band", -1)
    field_total = None
    for source_orbital, source_label in sources:
        weight = occupation(source_label, orbital_count)
        contribution = pair_contribution(
            target, source_orbital.reshape(grid_size, grid_size, grid_size), weight, hartley, kernel
        )
        contribution = contribution.reshape(1, grid_size, grid_size * grid_size)
        field_total = contribution if field_total is None else field_total + contribution
    field_total = lax.psum_scatter(
        field_total.astype(jnp.bfloat16), "group", scatter_dimension=1, tiled=True
    ).astype(jnp.float32)
    return -field_total


def solution(mesh):
    in_specs = (P("band", None, None), P(("band", "group"), None, None), P(("band", "group")), P())
    out_specs = P("band", "group", None)
    return jax.shard_map(shards, mesh=mesh, in_specs=in_specs, out_specs=out_specs, check_vma=False)
```

profile of v0, /device:TPU:1, one launch (start us, length us, event | category | flops | bytes accessed | tf_op | source)
XLA Modules:
  0.0 106.9 jit_solution(15902952215638397282)
XLA Ops:
  6.5 0.0 reduce-scatter.2.cloned.1.call-start
  6.5 20.5 %collective-permute-start.1 = (bf16[1,64,4096]{2,1,0:T(8,128)(2,1)}, bf16[1,64,4096]{2,1,0:T(8,128)(2,1)}, u32[]{:S(2)}, u32[]{:S(2)}) collective-permute-start(bf16[1,64,4096]{2,1,0:T(8,128)(2,1)} %param.5), channel_id=1, source_target_pairs={{0,764},{4,0},{8,4},{12,8},{16,12},{20,16},{24,20},{28,24},{32,28}... | collective-permute-start | bytes 1572872 | tf_op jit(solution)/shard_map/ppermute | solution.py:15
  27.0 3.0 %collective-permute-start = (s32[1]{0:T(128)}, s32[1]{0:T(128)}, u32[]{:S(2)}, u32[]{:S(2)}) collective-permute-start(s32[1]{0:T(128)} %param.6), channel_id=1, source_target_pairs={{0,764},{4,0},{8,4},{12,8},{16,12},{20,16},{24,20},{28,24},{32,28}... | collective-permute-start | bytes 20 | tf_op jit(solution)/shard_map/ppermute | solution.py:15
  30.0 1.3 %convert_multiply_fusion = f32[64,4096]{1,0:T(8,128)S(1)} fusion(s32[64,4096]{1,0:T(8,128)} %param.7), kind=kLoop, calls=%fused_computation.23 | loop fusion | flops 524288 | bytes 2097152 | tf_op jit(solution)/shard_map/mul | solution.py:34
  31.3 1.9 %reshape.112 = f32[64,64,64]{2,1,0:T(8,128)S(1)} reshape(bf16[1,64,4096]{2,1,0:T(8,128)(2,1)} %param.5) | data formatting | bytes 1572864 | tf_op jit(solution)/shard_map/convert_element_type | solution.py:52
  33.9 3.0 %reshape.111 = f32[64,64,64]{2,1,0:T(8,128)} reshape(bf16[1,64,4096]{2,1,0:T(8,128)(2,1)} %param.4) | data formatting | bytes 1572864 | tf_op jit(solution)/shard_map/convert_element_type | solution.py:52
  36.9 2.1 %mul.166 = f32[64,64,64]{2,1,0:T(8,128)} reshape(f32[64,4096]{1,0:T(8,128)S(1)} %convert_multiply_fusion) | data formatting | bytes 2097152 | tf_op jit(solution)/shard_map/mul | solution.py:34
  39.2 0.1 broadcast_add_fusion
  39.2 0.0 collective-permute-done
  40.0 0.0 collective-permute-done.1
  40.0 3.0 %reshape.115 = f32[64,64,64]{2,1,0:T(8,128)} reshape(bf16[1,64,4096]{2,1,0:T(8,128)(2,1)} %collective-permute-done.1) | data formatting | bytes 1572864 | tf_op jit(solution)/shard_map/convert_element_type | solution.py:52
  43.1 4.0 %multiply_convert_fusion.1 = (bf16[64,64,64]{2,1,0:T(8,128)(2,1)}, bf16[64,64,64]{2,1,0:T(8,128)(2,1)S(1)}) fusion(f32[64,64,64]{2,1,0:T(8,128)} %reshape.111, f32[64,64,64]{2,1,0:T(8,128)} %reshape.115, f32[64,64,64]{2,1,0:T(8,128)S(1)} %reshape.112), kind=kLoop, calls=%fused_computation.2 | loop fusion | flops 1048576 | bytes 4194304 | tf_op jit(solution)/shard_map/convert_element_type | solution.py:52
  47.1 0.0 copy-start
  47.1 1.1 convolution_convert_fusion.7
  48.1 1.1 convolution_convert_fusion.6
  49.2 0.0 copy-done
  49.2 1.5 %multiply_convert_fusion.2 = bf16[64,64,64]{2,1,0:T(8,128)(2,1)S(1)} fusion(bf16[64,64,64]{2,1,0:T(8,128)(2,1)S(1)} %convolution_convert_fusion.6, f32[64,64,64]{2,1,0:T(8,128)S(1)} %copy-done, s32[64]{0:T(128)S(1)} %fusion.64, s32[64,64]{1,0:T(8,128)S(1)} %broadcast_add_fusion), kind=kOutput, calls=%fused_computation.3 | convolution fusion | flops 35196928 | bytes 2113792 | tf_op jit(solution)/shard_map/dot_general | solution.py:46
  50.7 2.1 %convolution_convert_fusion.5 = bf16[64,64,64]{2,1,0:T(8,128)(2,1)} fusion(bf16[64,64,64]{2,1,0:T(8,128)(2,1)S(1)} %multiply_convert_fusion.2), kind=kOutput, calls=%fused_computation.11 | convolution fusion | flops 33886208 | bytes 1048576 | tf_op jit(solution)/shard_map/dot_general | solution.py:46
  52.8 3.5 %copy.9 = bf16[64,64,64]{0,1,2:T(8,128)(2,1)S(1)} copy(bf16[64,64,64]{2,1,0:T(8,128)(2,1)} %convolution_convert_fusion.5) | data formatting | bytes 1048576 | tf_op jit(solution)/shard_map/convert_element_type | solution.py:56
  56.3 2.9 %fusion = f32[64,64,64]{2,1,0:T(8,128)} fusion(bf16[64,64,64]{0,1,2:T(8,128)(2,1)S(1)} %copy.9), kind=kOutput, calls=%fused_computation.14 | convolution fusion | flops 67510272 | bytes 1572864 | tf_op jit(solution)/shard_map/dot_general | solution.py:46
  59.1 0.0 copy-start.1
  59.2 2.4 %convolution_convert_fusion.3 = bf16[64,64,64]{2,1,0:T(8,128)(2,1)S(1)} fusion(bf16[64,64,64]{2,1,0:T(8,128)(2,1)} %get-tuple-element.5), kind=kOutput, calls=%fused_computation.9 | convolution fusion | flops 33886208 | bytes 1048576 | tf_op jit(solution)/shard_map/dot_general | solution.py:46
  61.6 1.1 convolution_convert_fusion.2
  62.7 0.0 copy-done.1
  62.7 1.5 %multiply_convert_fusion = bf16[64,64,64]{2,1,0:T(8,128)(2,1)S(1)} fusion(bf16[64,64,64]{2,1,0:T(8,128)(2,1)S(1)} %convolution_convert_fusion.2, f32[64,64,64]{2,1,0:T(8,128)S(1)} %copy-done.1, s32[64]{0:T(128)S(1)} %fusion.64, s32[64,64]{1,0:T(8,128)S(1)} %broadcast_add_fusion), kind=kOutput, calls=%fused_computation.1 | convolution fusion | flops 35196928 | bytes 2113792 | tf_op jit(solution)/shard_map/dot_general | solution.py:46
  64.2 2.1 %convolution_convert_fusion.1 = bf16[64,64,64]{2,1,0:T(8,128)(2,1)} fusion(bf16[64,64,64]{2,1,0:T(8,128)(2,1)S(1)} %multiply_convert_fusion), kind=kOutput, calls=%fused_computation.7 | convolution fusion | flops 33886208 | bytes 1048576 | tf_op jit(solution)/shard_map/dot_general | solution.py:46
  66.3 3.3 %copy.14 = bf16[64,64,64]{0,1,2:T(8,128)(2,1)S(1)} copy(bf16[64,64,64]{2,1,0:T(8,128)(2,1)} %convolution_convert_fusion.1) | data formatting | bytes 1048576 | tf_op jit(solution)/shard_map/convert_element_type | solution.py:56
  69.6 4.9 %add_convert_fusion = bf16[64,64,64]{2,1,0:T(8,128)(2,1)} fusion(f32[64,64,64]{2,1,0:T(8,128)} %reshape.115, f32[64,64,64]{2,1,0:T(8,128)S(1)} %reshape.112, f32[64,64,64]{2,1,0:T(8,128)} %fusion, bf16[64,64,64]{0,1,2:T(8,128)(2,1)S(1)} %copy.14, f32[]{:T(128)} %bitcast.2, f32[]{:T(128)} %bitcast), kind=kOutput, calls=%fused_computation | convolution fusion | flops 69083136 | bytes 4194312 | tf_op jit(solution)/shard_map/dot_general | solution.py:46
  74.5 2.7 %convert_element_type.164 = bf16[1,64,4096]{2,1,0:T(8,128)(2,1)} reshape(bf16[64,64,64]{2,1,0:T(8,128)(2,1)} %add_convert_fusion) | data formatting | bytes 1048576 | tf_op jit(solution)/shard_map/convert_element_type | solution.py:83
  77.2 0.0 reduce-scatter.2.cloned.1.call-update
  77.2 21.2 %reduce-scatter.2.cloned.1.call-done = bf16[1,16,4096]{2,1,0:T(8,128)(2,1)} async-done(((bf16[1,64,4096]{2,1,0:T(8,128)(2,1)}), bf16[1,16,4096]{2,1,0:T(8,128)(2,1)}) %reduce-scatter.2.cloned.1.call-update) | async-done | bytes 131088 | tf_op jit(solution)/shard_map/reduce_scatter | solution.py:82
  98.5 1.6 %convert_negate_fusion = f32[1,16,4096]{2,1,0:T(8,128)} fusion(bf16[1,16,4096]{2,1,0:T(8,128)(2,1)} %reduce-scatter.2.cloned.1.call-done), kind=kLoop, calls=%fused_computation.24 | loop fusion | flops 131072 | bytes 393216 | tf_op jit(solution)/shard_map/neg | solution.py:85
  (1 shorter events, 0.0 us)
Async XLA Ops:
  6.5 91.9 %reduce-scatter.2.cloned.1.call-start = ((), (), s32[]{:S(2)}) async-start(), calls=%async_computation.1 | async-start | bytes 655360 | tf_op jit(solution)/shard_map/reduce_scatter | solution.py:82
  6.5 33.5 %collective-permute-start.1 = (bf16[1,64,4096]{2,1,0:T(8,128)(2,1)}, bf16[1,64,4096]{2,1,0:T(8,128)(2,1)}, u32[]{:S(2)}, u32[]{:S(2)}) collective-permute-start(bf16[1,64,4096]{2,1,0:T(8,128)(2,1)} %param.5), channel_id=1, source_target_pairs={{0,764},{4,0},{8,4},{12,8},{16,12},{20,16},{24,20},{28,24},{32,28}... | collective-permute-start | bytes 1572872 | tf_op jit(solution)/shard_map/ppermute | solution.py:15
  27.0 12.2 %collective-permute-start = (s32[1]{0:T(128)}, s32[1]{0:T(128)}, u32[]{:S(2)}, u32[]{:S(2)}) collective-permute-start(s32[1]{0:T(128)} %param.6), channel_id=1, source_target_pairs={{0,764},{4,0},{8,4},{12,8},{16,12},{20,16},{24,20},{28,24},{32,28}... | collective-permute-start | bytes 20 | tf_op jit(solution)/shard_map/ppermute | solution.py:15
  47.1 2.1 %copy-start = (f32[64,64,64]{2,1,0:T(8,128)S(1)}, f32[64,64,64]{2,1,0:T(8,128)}, u32[]{:S(2)}) copy-start(f32[64,64,64]{2,1,0:T(8,128)} %mul.166) | copy-start | bytes 3145732
  59.1 3.5 %copy-start.1 = (f32[64,64,64]{2,1,0:T(8,128)S(1)}, f32[64,64,64]{2,1,0:T(8,128)}, u32[]{:S(2)}) copy-start(f32[64,64,64]{2,1,0:T(8,128)} %mul.166) | copy-start | bytes 3145732
Sparse Core Ops, SparseCore 0:
  77.4 21.0 reduce-scatter.1
where the time goes:
time: 107 us
  starting transfers between devices  23.5 us (22%)
  waiting for transfers between devices  21.2 us (20%)
  matrix products  20.6 us (19%)
  local copies, waits for them, and re-layouts  19.6 us (18%)
  between operations  15 us (14%)
  other arithmetic  7.01 us (7%)
    ppermute x2, starting transfers between devices, passed_along(): return lax.ppermute(value, axis, pairs)  23.5 us
    reduce_scatter x1, waiting for transfers between devices, shards(): lax.psum_scatter(field_total.astype(jnp.bfloat16), 'group', scatter_dimen...  21.2 us
    dot_general x10, matrix products, axis_pass(): lax.dot_general(field_data, hartley, (((0,), (0,)), ((), ())), preferred_...  20.6 us
    convert_element_type x2, local copies, waits for them, and re-layouts, pair_contribution(): back_first = axis_pass(spectrum, hartley).astype(jnp.bfloat16)  6.78 us
    convert_element_type x2, local copies, waits for them, and re-layouts, pair_contribution(): source_orbital.astype(jnp.float32)  4.97 us
    convert_element_type x1, other arithmetic, pair_contribution(): (target.astype(jnp.float32) * source_orbital.astype(jnp.float32)).astype(...  4 us
    convert_element_type x1, local copies, waits for them, and re-layouts, pair_contribution(): target.astype(jnp.float32) * source_orbital.astype(jnp.float32)  3.01 us
    convert_element_type x1, local copies, waits for them, and re-layouts, shards(): field_total.astype(jnp.bfloat16)  2.7 us
  transfers between devices with their start and end apart: 3, of which 1 were waited for; matrix products, arithmetic and copies ran while one was open for 8% of the time, Pallas kernels for 0%

commit v1 on v0

v1 whole, which is shorter than its diff:
```python
import functools

import jax
import jax.numpy as jnp
import numpy as np
from jax import lax
from jax.experimental import pallas as pl
from jax.experimental.pallas import tpu as pltpu
from jax.sharding import PartitionSpec as P

WINDOW = 2
SCREEN_SQUARE = 16.0
N = 64
HALF = 32
LANES = 128
WIDE = 256
BLOCKS = N * N // WIDE


def cas_table():
    k = np.arange(N)
    angle = (k[:, None] * k[None, :] % N).astype(np.float64) * (2.0 * np.pi / N)
    return (np.cos(angle) + np.sin(angle)) / np.sqrt(float(N))


def tables():
    h = cas_table()
    order = np.concatenate([np.arange(0, N, 2), np.arange(1, N, 2)])
    diagonal = np.kron(np.eye(WIDE // N), h)
    return tuple(jnp.asarray(m, jnp.bfloat16) for m in (h, h[order], h[:, order], diagonal, np.eye(N)[order]))


def dot(a, b):
    return jnp.dot(a, b, preferred_element_type=jnp.float32)


def low_lanes():
    return lax.broadcasted_iota(jnp.int32, (HALF, LANES), 1) < N


def exchange(top, bottom, low):
    return (
        jnp.where(low, top, pltpu.roll(bottom, N, 1)),
        jnp.where(low, pltpu.roll(top, N, 1), bottom),
    )


def scatter_rows(block, column, turned, low):
    first, second = exchange(block[:HALF], block[HALF:], low)
    turned[pl.ds(2 * column, HALF, stride=N), :] = first
    turned[pl.ds(2 * column + 1, HALF, stride=N), :] = second


def gather_rows(column, turned, low):
    first = turned[pl.ds(2 * column, HALF, stride=N), :]
    second = turned[pl.ds(2 * column + 1, HALF, stride=N), :]
    top, bottom = exchange(first, second, low)
    return jnp.concatenate([top, bottom], axis=0)


def pair_field(target, source, scale, kernel, h, h_rows, h_cols, h_diag, turned, emit):
    low = low_lanes()
    for block in range(BLOCKS):
        columns = slice(block * WIDE, (block + 1) * WIDE)
        density = (
            target[:, columns].astype(jnp.float32) * source[:, columns].astype(jnp.float32)
        ).astype(jnp.bfloat16)
        first = dot(h_rows[...], density)
        for part in range(2):
            scatter_rows(first[:, part * LANES : (part + 1) * LANES], 2 * block + part, turned, low)
    for block in range(BLOCKS):
        rows = [slice((2 * block + part) * N, (2 * block + part + 1) * N) for part in range(2)]
        first = jnp.concatenate([turned[r, :].astype(jnp.bfloat16) for r in rows], axis=1)
        second = dot(h[...], first).astype(jnp.bfloat16)
        spectrum = dot(second, h_diag[...]) * kernel[:, block * WIDE : (block + 1) * WIDE]
        back = dot(spectrum.astype(jnp.bfloat16), h_diag[...]).astype(jnp.bfloat16)
        back = dot(h[...], back)
        for part in range(2):
            turned[rows[part], :] = back[:, part * LANES : (part + 1) * LANES]
    for block in range(BLOCKS):
        columns = slice(block * WIDE, (block + 1) * WIDE)
        back = jnp.concatenate(
            [gather_rows(2 * block + part, turned, low) for part in range(2)], axis=1
        ).astype(jnp.bfloat16)
        potential = dot(h_cols[...], back)
        emit(columns, potential * scale * source[:, columns].astype(jnp.float32))


def minus_occupation(label, count):
    shifted = (jnp.full((1, WIDE), label, jnp.int32).astype(jnp.float32) - count / 2.0) / (count / 4.0)
    return -1.0 / (1.0 + jnp.exp(shifted))


def own_kernel(count, label, target, source, mask, h, h_rows, h_cols, h_diag, rows, field, kernel, turned):
    low = low_lanes()
    for block in range(BLOCKS):
        kept = mask[:, block * WIDE : (block + 1) * WIDE].astype(jnp.float32).astype(jnp.bfloat16)
        kept = dot(rows[...], kept)
        for part in range(2):
            scatter_rows(kept[:, part * LANES : (part + 1) * LANES], 2 * block + part, turned, low)
    ky = lax.broadcasted_iota(jnp.int32, (N, LANES), 0)
    lane = lax.broadcasted_iota(jnp.int32, (N, LANES), 1)

    def squared(k):
        signed = jnp.where(k < N // 2, k, k - N)
        return signed * signed

    plane = squared(ky) + squared(lane % N)
    for half in range(HALF):
        q_square = plane + squared(2 * half + lane // N)
        kept = turned[half * N : (half + 1) * N, :]
        kernel[:, half * LANES : (half + 1) * LANES] = (
            kept * SCREEN_SQUARE / (q_square.astype(jnp.float32) + SCREEN_SQUARE)
        )

    def emit(columns, value):
        field[:, columns] = value

    pair_field(target, source, minus_occupation(label[0], count), kernel, h, h_rows, h_cols, h_diag, turned, emit)


def cross_kernel(count, label, target, source, field, kernel, h, h_rows, h_cols, h_diag, total, turned):
    def emit(columns, value):
        total[:, columns] = (field[:, columns] + value).astype(jnp.bfloat16)

    pair_field(target, source, minus_occupation(label[0], count), kernel, h, h_rows, h_cols, h_diag, turned, emit)


def call(kernel, outs, flops, name, *args):
    vmem = pl.BlockSpec(memory_space=pltpu.VMEM)
    return pl.pallas_call(
        kernel,
        out_shape=outs,
        in_specs=[pl.BlockSpec(memory_space=pltpu.SMEM)] + [vmem] * (len(args) - 1),
        out_specs=jax.tree.map(lambda _: vmem, outs),
        scratch_shapes=[pltpu.VMEM((HALF * N, LANES), jnp.float32)],
        compiler_params=pltpu.CompilerParams(vmem_limit_bytes=24 * 1024 * 1024),
        cost_estimate=pl.CostEstimate(flops=flops, bytes_accessed=4 * 1024 * 1024, transcendentals=0),
        name=name,
    )(*args)


def passed_along(value, axis, steps):
    count = lax.axis_size(axis)
    return lax.ppermute(value, axis, [(s, (s + steps) % count) for s in range(count)])


def shards(trial, orbitals, labels, kernel_mask):
    count = lax.axis_size("band") * lax.axis_size("group")
    members = lax.axis_size("group")
    *h, rows = tables()
    target, source = trial[0], orbitals[0]
    next_source = passed_along(source, "band", -1)
    next_label = passed_along(labels, "band", -1)
    plane = jax.ShapeDtypeStruct((N, N * N), jnp.float32)
    flops = 6 * 2 * N**4
    field, kernel = call(
        functools.partial(own_kernel, count), (plane, plane), flops, "own", labels, target, source, kernel_mask, *h, rows
    )
    total = call(
        functools.partial(cross_kernel, count),
        jax.ShapeDtypeStruct((N, N * N), jnp.bfloat16),
        flops,
        "cross",
        next_label, target, next_source, field, kernel, *h,
    )
    slabs = total.reshape(members, N // members, N * N)
    pieces = lax.all_to_all(slabs, "group", 0, 0)
    return jnp.sum(pieces.astype(jnp.float32), axis=0, keepdims=True)


def solution(mesh):
    in_specs = (P("band", None, None), P(("band", "group"), None, None), P(("band", "group")), P())
    out_specs = P("band", "group", None)
    return jax.shard_map(shards, mesh=mesh, in_specs=in_specs, out_specs=out_specs, check_vma=False)
```

time: 107 us -> 57.7 us (0.54)
  waiting for transfers between devices: 21.2 us -> 0.01 us
  matrix products: 20.6 us -> 0 us
  between operations: 15 us -> 0.73 us
  Pallas kernels: 0 us -> 13.7 us
  local copies, waits for them, and re-layouts: 19.6 us -> 7.07 us
  blocking collectives: 0 us -> 11.4 us
  other arithmetic: 7.01 us -> 0.77 us
    reduce_scatter x1 -> x0, waiting for transfers between devices: 21.2 us -> none  [shards(): lax.psum_scatter(field_total.astype(jnp.bfloat16), 'group', scatter_dimen...]
    dot_general x10 -> x0, matrix products: 20.6 us -> none  [axis_pass(): lax.dot_general(field_data, hartley, (((0,), (0,)), ((), ())), preferred_...]
    convert_element_type x6 -> x0, local copies, waits for them, and re-layouts: 17.5 us -> none  [the longest x2 6.78 us: pair_contribution(): back_first = axis_pass(spectrum, hartley).astype(jnp.bfloat16)]
    pallas_call x0 -> x2, Pallas kernels: none -> 13.7 us  [call(): pl.pallas_call(kernel, out_shape=outs, in_specs=[pl.BlockSpec(memory_spac...]
    all_to_all x0 -> x1, blocking collectives: none -> 11.4 us  [shards(): pieces = lax.all_to_all(slabs, 'group', 0, 0)]
    unnamed x4 -> x16, local copies, waits for them, and re-layouts: 0.01 us -> 7.07 us
    convert_element_type x1 -> x0, other arithmetic: 4 us -> none  [pair_contribution(): (target.astype(jnp.float32) * source_orbital.astype(jnp.float32)).astype(...]
    mul x1 -> x0, local copies, waits for them, and re-layouts: 2.14 us -> none  [screened_kernel(): mask_cube.astype(jnp.float32) * screen_square]
  transfers between devices with their start and end apart: 3 -> 2, of which waited for: 1 -> 0; matrix products, arithmetic and copies ran while one was open for 8% -> 0% of each run, Pallas kernels for 0% -> 12%
where the time goes in v1:
time: 57.7 us; the launch traced here: 57.1 us
  starting transfers between devices  23.5 us (41%)
  Pallas kernels  13.7 us (24%)
  blocking collectives  11.4 us (20%)
  local copies, waits for them, and re-layouts  7.07 us (12%)
  other arithmetic  0.77 us (1%)
  between operations  0.73 us (1%)
    ppermute x2, starting transfers between devices, passed_along(): lax.ppermute(value, axis, [(s, (s + steps) % count) for s in range(count)])  23.5 us
    pallas_call x2, Pallas kernels, call(): pl.pallas_call(kernel, out_shape=outs, in_specs=[pl.BlockSpec(memory_spac...  13.7 us
    all_to_all x1, blocking collectives, shards(): pieces = lax.all_to_all(slabs, 'group', 0, 0)  11.4 us
    unnamed x16, local copies, waits for them, and re-layouts  7.07 us
  transfers between devices with their start and end apart: 2, of which 0 were waited for; matrix products, arithmetic and copies ran while one was open for 0% of the time, Pallas kernels for 12%

profile of v1, /device:TPU:1, one launch (start us, length us, event | category | flops | bytes accessed | tf_op | source)
XLA Modules:
  0.0 57.1 jit_solution(15813048829495526300)
XLA Ops:
  0.0 20.5 %collective-permute-start.1 = (bf16[64,4096]{1,0:T(8,128)(2,1)}, bf16[64,4096]{1,0:T(8,128)(2,1)S(1)}, u32[]{:S(2)}, u32[]{:S(2)}) collective-permute-start(bf16[64,4096]{1,0:T(8,128)(2,1)} %bitcast.7), channel_id=1, source_target_pairs={{0,764},{4,0},{8,4},{12,8},{16,12},{20,16},{24,20},{28,24},{32,28}... | collective-permute-start | bytes 1572872 | tf_op jit(solution)/shard_map/ppermute | solution.py:145
  20.5 3.0 %collective-permute-start = (s32[1]{0:T(128)}, s32[1]{0:T(128)}, u32[]{:S(2)}, u32[]{:S(2)}) collective-permute-start(s32[1]{0:T(128)} %param.11), channel_id=1, source_target_pairs={{0,764},{4,0},{8,4},{12,8},{16,12},{20,16},{24,20},{28,24},{32,28}... | collective-permute-start | bytes 20 | tf_op jit(solution)/shard_map/ppermute | solution.py:145
  24.1 0.0 copy-start
  24.1 1.0 %copy-done = bf16[1,64,4096]{2,1,0:T(8,128)(2,1)S(1)} copy-done((bf16[1,64,4096]{2,1,0:T(8,128)(2,1)S(1)}, bf16[1,64,4096]{2,1,0:T(8,128)(2,1)}, u32[]{:S(2)}) %copy-start) | copy-done | bytes 524312
  25.2 0.0 copy-start.1
  25.2 1.2 %copy-done.1 = s32[64,4096]{1,0:T(8,128)S(1)} copy-done((s32[64,4096]{1,0:T(8,128)S(1)}, s32[64,4096]{1,0:T(8,128)}, u32[]{:S(2)}) %copy-start.1) | copy-done | bytes 1048600
  26.4 0.0 copy-start.2
  26.4 1.0 %copy-done.2 = bf16[1,64,4096]{2,1,0:T(8,128)(2,1)S(1)} copy-done((bf16[1,64,4096]{2,1,0:T(8,128)(2,1)S(1)}, bf16[1,64,4096]{2,1,0:T(8,128)(2,1)}, u32[]{:S(2)}) %copy-start.2) | copy-done | bytes 524312
  27.4 0.0 copy-start.3
  27.4 0.9 %copy-done.3 = bf16[256,256]{1,0:T(8,128)(2,1)S(1)} copy-done((bf16[256,256]{1,0:T(8,128)(2,1)S(1)}, bf16[256,256]{1,0:T(8,128)(2,1)}, u32[]{:S(2)}) %copy-start.3) | copy-done | bytes 131096
  28.3 0.0 copy-start.4
  28.4 0.7 %copy-done.4 = bf16[64,64]{1,0:T(8,128)(2,1)S(1)} copy-done((bf16[64,64]{1,0:T(8,128)(2,1)S(1)}, bf16[64,64]{1,0:T(8,128)(2,1)}, u32[]{:S(2)}) %copy-start.4) | copy-done | bytes 8216
  29.1 0.0 copy-start.5
  29.1 0.7 %copy-done.5 = bf16[64,64]{1,0:T(8,128)(2,1)S(1)} copy-done((bf16[64,64]{1,0:T(8,128)(2,1)S(1)}, bf16[64,64]{1,0:T(8,128)(2,1)}, u32[]{:S(2)}) %copy-start.5) | copy-done | bytes 8216
  29.8 0.0 copy-start.6
  29.8 0.7 %copy-done.6 = bf16[64,64]{1,0:T(8,128)(2,1)S(1)} copy-done((bf16[64,64]{1,0:T(8,128)(2,1)S(1)}, bf16[64,64]{1,0:T(8,128)(2,1)}, u32[]{:S(2)}) %copy-start.6) | copy-done | bytes 8216
  30.5 0.0 copy-start.7
  30.5 0.7 %copy-done.7 = bf16[64,64]{1,0:T(8,128)(2,1)S(1)} copy-done((bf16[64,64]{1,0:T(8,128)(2,1)S(1)}, bf16[64,64]{1,0:T(8,128)(2,1)}, u32[]{:S(2)}) %copy-start.7) | copy-done | bytes 8216
  31.2 6.8 %own.1 = (f32[64,4096]{1,0:T(8,128)S(1)}, f32[64,4096]{1,0:T(8,128)S(1)}) custom-call(s32[1]{0:T(128)S(6)} %copy.10.label, bf16[64,4096]{1,0:T(8,128)(2,1)S(1)} %bitcast.4, bf16[64,4096]{1,0:T(8,128)(2,1)S(1)} %bitcast.8, s32[64,4096]{1,0:T(8,128)S(1)} %copy-done.1, bf16[64,64]{1,0:T(8,128)(2,1)S(1)} %copy-done.6, bf16[64,64]{1,0:T(8,128)(2,1)S(1)} %copy-done.5, ...), custom_call_target="tpu_custom_call" | custom-call | flops 201326592 | bytes 4194304 | tf_op jit(solution)/shard_map/own/pallas_call | solution.py:131
  38.0 0.0 collective-permute-done.label
  38.1 0.0 collective-permute-done.1.source
  38.1 6.9 %cross.1 = bf16[64,4096]{1,0:T(8,128)(2,1)S(1)} custom-call(s32[1]{0:T(128)} %collective-permute-done.label, bf16[64,4096]{1,0:T(8,128)(2,1)S(1)} %bitcast.5, bf16[64,4096]{1,0:T(8,128)(2,1)S(1)} %collective-permute-done.1.source, f32[64,4096]{1,0:T(8,128)S(1)} %get-tuple-element.7.field, f32[64,4096]{1,0:T(8,128)S(1)} %get-tuple-element.8.kernel, ...), custom_call_target="tpu_custom_call" | custom-call | flops 201326592 | bytes 4194304 | tf_op jit(solution)/shard_map/cross/pallas_call | solution.py:131
  44.9 11.4 %all_to_all.5 = bf16[4,16,4096]{2,1,0:T(8,128)(2,1)S(1)} all-to-all(bf16[4,16,4096]{2,1,0:T(8,128)(2,1)S(1)} %bitcast.6), channel_id=1, replica_groups=mesh['band'=192,'group'=4] {'group'}, dimensions={0} | all-to-all | bytes 1048576 | tf_op jit(solution)/shard_map/all_to_all | solution.py:168
  56.4 0.8 %convert_reduce_fusion = f32[16,4096]{1,0:T(8,128)} fusion(bf16[4,16,4096]{2,1,0:T(8,128)(2,1)S(1)} %all_to_all.5), kind=kLoop, calls=%fused_computation | loop fusion | flops 458752 | bytes 786432 | tf_op jit(solution)/shard_map/reduce_sum | solution.py:169
Async XLA Ops:
  0.0 38.1 %collective-permute-start.1 = (bf16[64,4096]{1,0:T(8,128)(2,1)}, bf16[64,4096]{1,0:T(8,128)(2,1)S(1)}, u32[]{:S(2)}, u32[]{:S(2)}) collective-permute-start(bf16[64,4096]{1,0:T(8,128)(2,1)} %bitcast.7), channel_id=1, source_target_pairs={{0,764},{4,0},{8,4},{12,8},{16,12},{20,16},{24,20},{28,24},{32,28}... | collective-permute-start | bytes 1572872 | tf_op jit(solution)/shard_map/ppermute | solution.py:145
  20.5 17.6 %collective-permute-start = (s32[1]{0:T(128)}, s32[1]{0:T(128)}, u32[]{:S(2)}, u32[]{:S(2)}) collective-permute-start(s32[1]{0:T(128)} %param.11), channel_id=1, source_target_pairs={{0,764},{4,0},{8,4},{12,8},{16,12},{20,16},{24,20},{28,24},{32,28}... | collective-permute-start | bytes 20 | tf_op jit(solution)/shard_map/ppermute | solution.py:145
  24.1 1.0 %copy-start = (bf16[1,64,4096]{2,1,0:T(8,128)(2,1)S(1)}, bf16[1,64,4096]{2,1,0:T(8,128)(2,1)}, u32[]{:S(2)}) copy-start(bf16[1,64,4096]{2,1,0:T(8,128)(2,1)} %param.9) | copy-start | bytes 1572868
  25.2 1.2 %copy-start.1 = (s32[64,4096]{1,0:T(8,128)S(1)}, s32[64,4096]{1,0:T(8,128)}, u32[]{:S(2)}) copy-start(s32[64,4096]{1,0:T(8,128)} %mask.1) | copy-start | bytes 3145732
  26.4 1.0 %copy-start.2 = (bf16[1,64,4096]{2,1,0:T(8,128)(2,1)S(1)}, bf16[1,64,4096]{2,1,0:T(8,128)(2,1)}, u32[]{:S(2)}) copy-start(bf16[1,64,4096]{2,1,0:T(8,128)(2,1)} %param.10) | copy-start | bytes 1572868
  27.4 0.9 %copy-start.3 = (bf16[256,256]{1,0:T(8,128)(2,1)S(1)}, bf16[256,256]{1,0:T(8,128)(2,1)}, u32[]{:S(2)}) copy-start(bf16[256,256]{1,0:T(8,128)(2,1)} %constant.15.clone.h_diag) | copy-start | bytes 393220
  28.3 0.7 %copy-start.4 = (bf16[64,64]{1,0:T(8,128)(2,1)S(1)}, bf16[64,64]{1,0:T(8,128)(2,1)}, u32[]{:S(2)}) copy-start(bf16[64,64]{1,0:T(8,128)(2,1)} %constant.14.clone.h_cols) | copy-start | bytes 24580
  29.1 0.7 %copy-start.5 = (bf16[64,64]{1,0:T(8,128)(2,1)S(1)}, bf16[64,64]{1,0:T(8,128)(2,1)}, u32[]{:S(2)}) copy-start(bf16[64,64]{1,0:T(8,128)(2,1)} %constant.13.clone.h_rows) | copy-start | bytes 24580
  29.8 0.7 %copy-start.6 = (bf16[64,64]{1,0:T(8,128)(2,1)S(1)}, bf16[64,64]{1,0:T(8,128)(2,1)}, u32[]{:S(2)}) copy-start(bf16[64,64]{1,0:T(8,128)(2,1)} %constant.12.clone.h) | copy-start | bytes 24580
  30.5 0.7 %copy-start.7 = (bf16[64,64]{1,0:T(8,128)(2,1)S(1)}, bf16[64,64]{1,0:T(8,128)(2,1)}, u32[]{:S(2)}) copy-start(bf16[64,64]{1,0:T(8,128)(2,1)} %constant.16.clone.rows) | copy-start | bytes 24580

commit v2 on v1

v2 whole, which is shorter than its diff:
```python
import functools

import jax
import jax.numpy as jnp
import numpy as np
from jax import lax
from jax.experimental import pallas as pl
from jax.experimental.pallas import tpu as pltpu
from jax.sharding import PartitionSpec as P

SCREEN_SQUARE = 16.0
N = 64
HALF = 32
LANES = 128
WIDE = 256
BLOCKS = N * N // WIDE
STRIDE = 65
CHUNK = 256
MEMBERS = 4
SLAB = N // MEMBERS

DIAG, CAS, CAS_ROWS, CAS_COLS, EVEN_FIRST, TABLE_ROWS = 0, 256, 320, 384, 448, 512


def tables():
    k = np.arange(N)
    angle = (k[:, None] * k[None, :] % N).astype(np.float64) * (2.0 * np.pi / N)
    h = (np.cos(angle) + np.sin(angle)) / np.sqrt(float(N))
    order = np.concatenate([np.arange(0, N, 2), np.arange(1, N, 2)])
    table = np.zeros((TABLE_ROWS, WIDE))
    table[DIAG:CAS] = np.kron(np.eye(WIDE // N), h)
    table[CAS:CAS_ROWS, :N] = h
    table[CAS_ROWS:CAS_COLS, :N] = h[order]
    table[CAS_COLS:EVEN_FIRST, :N] = h[:, order]
    table[EVEN_FIRST:, :N] = np.eye(N)[order]
    return jnp.asarray(table, jnp.bfloat16)


def dot(a, b):
    return jnp.dot(a, b, preferred_element_type=jnp.float32)


def low_lanes():
    return lax.broadcasted_iota(jnp.int32, (HALF, LANES), 1) < N


def exchange(top, bottom, low):
    return (
        jnp.where(low, top, pltpu.roll(bottom, N, 1)),
        jnp.where(low, pltpu.roll(top, N, 1), bottom),
    )


def scatter_rows(block, column, turned, low):
    first, second = exchange(block[:HALF], block[HALF:], low)
    turned[pl.ds(2 * column, HALF, stride=STRIDE), :] = first
    turned[pl.ds(2 * column + 1, HALF, stride=STRIDE), :] = second


def gather_rows(column, turned, low):
    first = turned[pl.ds(2 * column, HALF, stride=STRIDE), :]
    second = turned[pl.ds(2 * column + 1, HALF, stride=STRIDE), :]
    top, bottom = exchange(first, second, low)
    return jnp.concatenate([top, bottom], axis=0)


def turned_block(block, turned):
    return jnp.concatenate(
        [turned[pl.ds((2 * block + part) * STRIDE, N), :].astype(jnp.bfloat16) for part in range(2)], axis=1
    )


def columns_of(block):
    return slice(block * WIDE, (block + 1) * WIDE)


def by_owner(me, ref, columns):
    return jnp.concatenate([ref[pl.ds((me ^ k) * SLAB, SLAB), columns] for k in range(MEMBERS)], axis=0)


def pair_field(me, target, source, scale, kernel_ready, table, turned, rows, emit):
    low = low_lanes()
    h_diag, h, h_rows = table[DIAG:CAS, :], table[CAS:CAS_ROWS, :N], table[CAS_ROWS:CAS_COLS, :N]
    for block in range(BLOCKS):
        first = dot(h_rows, target[:, columns_of(block)] * source[:, columns_of(block)])
        for part in range(2):
            scatter_rows(first[:, part * LANES : (part + 1) * LANES], 2 * block + part, turned, low)
    for block in range(BLOCKS):
        rows[block * N : (block + 1) * N, :] = dot(h, turned_block(block, turned)).astype(jnp.bfloat16)
    kernel = kernel_ready()
    for chunk in range(BLOCKS * N // CHUNK):
        part = slice(chunk * CHUNK, (chunk + 1) * CHUNK)
        spectrum = dot(rows[part, :], h_diag) * kernel[part, :]
        rows[part, :] = dot(spectrum.astype(jnp.bfloat16), h_diag).astype(jnp.bfloat16)
    for block in range(BLOCKS):
        back = dot(h, rows[block * N : (block + 1) * N, :])
        for part in range(2):
            turned[pl.ds((2 * block + part) * STRIDE, N), :] = back[:, part * LANES : (part + 1) * LANES]
    h_cols = by_owner(me, table.at[CAS_COLS:EVEN_FIRST], slice(0, N))
    for block in range(BLOCKS):
        back = jnp.concatenate(
            [gather_rows(2 * block + part, turned, low) for part in range(2)], axis=1
        ).astype(jnp.bfloat16)
        potential = dot(h_cols, back)
        emit(block, potential * scale * by_owner(me, source, columns_of(block)).astype(jnp.float32))


def own_kernel(count, label, target, source, mask, table, field, kernel, weight, target_out, table_out,
               source_in, mask_in, turned, rows, sems):
    copies = [
        pltpu.make_async_copy(a, b, sems.at[i])
        for i, (a, b) in enumerate(
            ((target, target_out), (source, source_in), (table, table_out), (mask, mask_in))
        )
    ]
    for copy in copies:
        copy.start()
    me = lax.axis_index("group")
    shifted = (jnp.full((8, LANES), label[0], jnp.int32).astype(jnp.float32) - count / 2.0) / (count / 4.0)
    scale = -1.0 / (1.0 + jnp.exp(shifted))
    weight[...] = scale
    low = low_lanes()
    ky = lax.broadcasted_iota(jnp.int32, (N, LANES), 0)
    lane = lax.broadcasted_iota(jnp.int32, (N, LANES), 1)

    def squared(k):
        signed = jnp.where(k < N // 2, k, k - N)
        return signed * signed

    plane = squared(ky) + squared(lane % N)

    for copy in copies:
        copy.wait()
    even_first = table_out[EVEN_FIRST:, :N]
    for block in range(BLOCKS):
        kept = dot(even_first, mask_in[:, columns_of(block)].astype(jnp.float32).astype(jnp.bfloat16))
        for part in range(2):
            scatter_rows(kept[:, part * LANES : (part + 1) * LANES], 2 * block + part, turned, low)
    for half in range(HALF):
        q_square = plane + squared(2 * half + lane // N)
        kept = turned[pl.ds(half * STRIDE, N), :]
        block, part = half // 2, half % 2
        kernel[block * N : (block + 1) * N, part * LANES : (part + 1) * LANES] = (
            kept * SCREEN_SQUARE / (q_square.astype(jnp.float32) + SCREEN_SQUARE)
        )

    def emit(block, value):
        field[:, columns_of(block)] = value

    pair_field(me, target_out, source_in, scale[:1, :1], lambda: kernel, table_out, turned, rows, emit)


def cross_kernel(weight, target, source, field, kernel, table, mine, *rest):
    sent, (turned, rows) = rest[: MEMBERS - 1], rest[MEMBERS - 1 :]

    def emit(block, value):
        total = field[:, columns_of(block)] + value
        mine[:, columns_of(block)] = total[:SLAB]
        for k in range(1, MEMBERS):
            sent[k - 1][:, columns_of(block)] = total[k * SLAB : (k + 1) * SLAB].astype(jnp.bfloat16)

    pair_field(
        lax.axis_index("group"), target, source, weight[:1, :1], lambda: kernel, table, turned, rows, emit
    )


def shape(rows, columns, dtype):
    return jax.ShapeDtypeStruct((rows, columns), dtype)


PAIR_SCRATCH = [pltpu.VMEM((HALF * STRIDE, LANES), jnp.float32), pltpu.VMEM((BLOCKS * N, WIDE), jnp.bfloat16)]
VMEM = pl.BlockSpec(memory_space=pltpu.VMEM)
HBM = pl.BlockSpec(memory_space=pltpu.HBM)


def call(kernel, outs, in_specs, scratch, name):
    return pl.pallas_call(
        kernel,
        out_shape=outs,
        in_specs=in_specs,
        out_specs=[VMEM] * len(outs),
        scratch_shapes=scratch,
        compiler_params=pltpu.CompilerParams(vmem_limit_bytes=40 * 1024 * 1024),
        cost_estimate=pl.CostEstimate(flops=6 * 2 * N**4, bytes_accessed=4 * 1024 * 1024, transcendentals=0),
        name=name,
    )


def passed_along(value, axis, steps):
    count = lax.axis_size(axis)
    return lax.ppermute(value, axis, [(s, (s + steps) % count) for s in range(count)])


def swapped(value, bits):
    return lax.ppermute(value, "group", [(s, s ^ bits) for s in range(MEMBERS)])


def shards(trial, orbitals, labels, kernel_mask):
    count = lax.axis_size("band") * lax.axis_size("group")
    target, source = trial[0], orbitals[0]
    next_source = passed_along(source, "band", -1)
    field, kernel, weight, target, table = call(
        functools.partial(own_kernel, count),
        (
            shape(N, N * N, jnp.float32),
            shape(BLOCKS * N, WIDE, jnp.float32),
            shape(8, LANES, jnp.float32),
            shape(N, N * N, jnp.bfloat16),
            shape(TABLE_ROWS, WIDE, jnp.bfloat16),
        ),
        [pl.BlockSpec(memory_space=pltpu.SMEM)] + [HBM] * 4,
        [pltpu.VMEM((N, N * N), jnp.bfloat16), pltpu.VMEM((N, N * N), jnp.int32)]
        + PAIR_SCRATCH
        + [pltpu.SemaphoreType.DMA((4,))],
        "own",
    )(labels, target, source, kernel_mask, tables())
    next_weight = passed_along(weight, "band", -1)
    mine, *sent = call(
        cross_kernel,
        [shape(SLAB, N * N, jnp.float32)] + [shape(SLAB, N * N, jnp.bfloat16)] * (MEMBERS - 1),
        [VMEM] * 6,
        PAIR_SCRATCH,
        "cross",
    )(next_weight, target, next_source, field, kernel, table)
    received = {bits: swapped(sent[bits - 1], bits) for bits in (2, 3, 1)}
    for bits in (2, 3, 1):
        mine = mine + received[bits].astype(jnp.float32)
    return mine[None]


def solution(mesh):
    in_specs = (P("band", None, None), P(("band", "group"), None, None), P(("band", "group")), P())
    out_specs = P("band", "group", None)
    return jax.shard_map(shards, mesh=mesh, in_specs=in_specs, out_specs=out_specs, check_vma=False)
```

time: 57.7 us -> 46.8 us (0.81)
  blocking collectives: 11.4 us -> 0 us
  Pallas kernels: 13.7 us -> 3.96 us
  starting transfers between devices: 23.5 us -> 32.9 us
  waiting for transfers between devices: 0.01 us -> 3.77 us
  local copies, waits for them, and re-layouts: 7.07 us -> 4.25 us
    all_to_all x1 -> x0, blocking collectives: 11.4 us -> none  [shards(): pieces = lax.all_to_all(slabs, 'group', 0, 0)]
    pallas_call x2, Pallas kernels: 13.7 us -> 3.96 us  [the longest x1 2.29 us: shards(): call(functools.partial(own_kernel, count), (shape(N, N * N, jnp.float32),...]
    ppermute x0 -> x3, starting transfers between devices: none -> 9.48 us  [swapped(): return lax.ppermute(value, 'group', [(s, s ^ bits) for s in range(MEMBERS)])]
    unnamed x16 -> x8, local copies, waits for them, and re-layouts: 7.07 us -> 4.25 us
    ppermute x0 -> x3, waiting for transfers between devices: none -> 2.39 us  [swapped(): return lax.ppermute(value, 'group', [(s, s ^ bits) for s in range(MEMBERS)])]
    ppermute x2, waiting for transfers between devices: 0.01 us -> 1.38 us  [passed_along(): lax.ppermute(value, axis, [(s, (s + steps) % count) for s in range(count)])]
    reduce_sum x1 -> x0, other arithmetic: 0.77 us -> none  [shards(): return jnp.sum(pieces.astype(jnp.float32), axis=0, keepdims=True)]
    broadcast_in_dim x0 -> x1, other arithmetic: none -> 0.76 us  [shards(): return mine[None]]
  transfers between devices with their start and end apart: 2 -> 5, of which waited for: 0 -> 2; matrix products, arithmetic and copies ran while one was open for 0% -> 0% of each run, Pallas kernels for 12% -> 5%
where the time goes in v2:
time: 46.8 us; the launch traced here: 46.4 us
  starting transfers between devices  32.9 us (70%)
  local copies, waits for them, and re-layouts  4.25 us (9%)
  Pallas kernels  3.96 us (8%)
  waiting for transfers between devices  3.77 us (8%)
  other arithmetic  0.76 us (2%)
  between operations  0.72 us (2%)
    ppermute x2, starting transfers between devices, passed_along(): lax.ppermute(value, axis, [(s, (s + steps) % count) for s in range(count)])  23.4 us
    ppermute x3, starting transfers between devices, swapped(): return lax.ppermute(value, 'group', [(s, s ^ bits) for s in range(MEMBERS)])  9.48 us
    unnamed x8, local copies, waits for them, and re-layouts  4.25 us
    ppermute x3, waiting for transfers between devices, swapped(): return lax.ppermute(value, 'group', [(s, s ^ bits) for s in range(MEMBERS)])  2.39 us
    pallas_call x1, Pallas kernels, shards(): call(functools.partial(own_kernel, count), (shape(N, N * N, jnp.float32),...  2.29 us
    pallas_call x1, Pallas kernels, shards(): call(cross_kernel, [shape(SLAB, N * N, jnp.float32)] + [shape(SLAB, N * N...  1.66 us
    ppermute x2, waiting for transfers between devices, passed_along(): lax.ppermute(value, axis, [(s, (s + steps) % count) for s in range(count)])  1.38 us
  transfers between devices with their start and end apart: 5, of which 2 were waited for; matrix products, arithmetic and copies ran while one was open for 0% of the time, Pallas kernels for 5%

profile of v2, /device:TPU:1, one launch (start us, length us, event | category | flops | bytes accessed | tf_op | source)
XLA Modules:
  0.0 46.4 jit_solution(6494335359846065477)
XLA Ops:
  0.0 20.5 %collective-permute-start.1 = (bf16[64,4096]{1,0:T(8,128)(2,1)}, bf16[64,4096]{1,0:T(8,128)(2,1)S(1)}, u32[]{:S(2)}, u32[]{:S(2)}) collective-permute-start(bf16[64,4096]{1,0:T(8,128)(2,1)} %bitcast.5), channel_id=1, source_target_pairs={{0,764},{4,0},{8,4},{12,8},{16,12},{20,16},{24,20},{28,24},{32,28}... | collective-permute-start | bytes 1572872 | tf_op jit(solution)/shard_map/ppermute | solution.py:191
  21.1 0.0 copy-start
  21.1 1.2 %copy-done = s32[64,4096]{1,0:T(8,128)S(1)} copy-done((s32[64,4096]{1,0:T(8,128)S(1)}, s32[64,4096]{1,0:T(8,128)}, u32[]{:S(2)}) %copy-start) | copy-done | bytes 1048600
  22.4 0.0 copy-start.1
  22.4 1.0 %copy-done.1 = bf16[1,64,4096]{2,1,0:T(8,128)(2,1)S(1)} copy-done((bf16[1,64,4096]{2,1,0:T(8,128)(2,1)S(1)}, bf16[1,64,4096]{2,1,0:T(8,128)(2,1)}, u32[]{:S(2)}) %copy-start.1) | copy-done | bytes 524312
  23.4 0.0 copy-start.2
  23.4 1.0 %copy-done.2 = bf16[1,64,4096]{2,1,0:T(8,128)(2,1)S(1)} copy-done((bf16[1,64,4096]{2,1,0:T(8,128)(2,1)S(1)}, bf16[1,64,4096]{2,1,0:T(8,128)(2,1)}, u32[]{:S(2)}) %copy-start.2) | copy-done | bytes 524312
  24.4 0.0 copy-start.3
  24.4 0.9 %copy-done.3 = bf16[512,256]{1,0:T(8,128)(2,1)S(1)} copy-done((bf16[512,256]{1,0:T(8,128)(2,1)S(1)}, bf16[512,256]{1,0:T(8,128)(2,1)}, u32[]{:S(2)}) %copy-start.3) | copy-done | bytes 262168
  25.4 2.3 %own.1 = (f32[64,4096]{1,0:T(8,128)S(1)}, f32[1024,256]{1,0:T(8,128)S(1)}, f32[8,128]{1,0:T(8,128)S(1)}, bf16[64,4096]{1,0:T(8,128)(2,1)S(1)}, bf16[512,256]{1,0:T(8,128)(2,1)S(1)}) custom-call(s32[1]{0:T(128)S(6)} %copy.6.label, bf16[64,4096]{1,0:T(8,128)(2,1)S(1)} %bitcast.4, bf16[64,4096]{1,0:T(8,128)(2,1)S(1)} %bitcast.6, s32[64,4096]{1,0:T(8,128)S(1)} %copy-done, ...), custom_call_target="tpu_custom_call" | custom-call | flops 201326592 | bytes 4194304 | tf_op jit(solution)/shard_map/own/pallas_call | solution.py:202
  27.7 3.0 %collective-permute-start = (f32[8,128]{1,0:T(8,128)S(1)}, f32[8,128]{1,0:T(8,128)S(1)}, u32[]{:S(2)}, u32[]{:S(2)}) collective-permute-start(f32[8,128]{1,0:T(8,128)S(1)} %get-tuple-element.14), channel_id=1, source_target_pairs={{0,764},{4,0},{8,4},{12,8},{16,12},{20,16},{24,20},{28,24},{32,28}... | collective-permute-start | bytes 12296 | tf_op jit(solution)/shard_map/ppermute | solution.py:191
  30.7 1.4 %collective-permute-done.weight = f32[8,128]{1,0:T(8,128)S(1)} collective-permute-done((f32[8,128]{1,0:T(8,128)S(1)}, f32[8,128]{1,0:T(8,128)S(1)}, u32[]{:S(2)}, u32[]{:S(2)}) %collective-permute-start) | collective-permute-done | bytes 4128 | tf_op jit(solution)/shard_map/ppermute | solution.py:191
  32.0 0.0 collective-permute-done.1.source
  32.0 1.7 %cross.1 = (f32[16,4096]{1,0:T(8,128)S(1)}, bf16[16,4096]{1,0:T(8,128)(2,1)S(1)}, bf16[16,4096]{1,0:T(8,128)(2,1)S(1)}, bf16[16,4096]{1,0:T(8,128)(2,1)S(1)}) custom-call(f32[8,128]{1,0:T(8,128)S(1)} %collective-permute-done.weight, bf16[64,4096]{1,0:T(8,128)(2,1)S(1)} %get-tuple-element.15.target, bf16[64,4096]{1,0:T(8,128)(2,1)S(1)} %collective-permute-done.1.source, ...), custom_call_target="tpu_custom_call" | custom-call | flops 201326592 | bytes 4194304 | tf_op jit(solution)/shard_map/cross/pallas_call | solution.py:218
  33.7 2.2 %collective-permute-start.2 = (bf16[16,4096]{1,0:T(8,128)(2,1)S(1)}, bf16[16,4096]{1,0:T(8,128)(2,1)S(1)}, u32[]{:S(2)}, u32[]{:S(2)}) collective-permute-start(bf16[16,4096]{1,0:T(8,128)(2,1)S(1)} %get-tuple-element.20), channel_id=1, source_target_pairs={{0,2},{1,3},{2,0},{3,1},{4,6},{5,7},{6,4},{7,5},{8,10},{9,11},{10,... | collective-permute-start | bytes 393224 | tf_op jit(solution)/shard_map/ppermute | solution.py:195
  35.9 5.3 %collective-permute-start.3 = (bf16[16,4096]{1,0:T(8,128)(2,1)S(1)}, bf16[16,4096]{1,0:T(8,128)(2,1)S(1)}, u32[]{:S(2)}, u32[]{:S(2)}) collective-permute-start(bf16[16,4096]{1,0:T(8,128)(2,1)S(1)} %get-tuple-element.21), channel_id=1, source_target_pairs={{0,3},{1,2},{2,1},{3,0},{4,7},{5,6},{6,5},{7,4},{8,11},{9,10},{10,... | collective-permute-start | bytes 393224 | tf_op jit(solution)/shard_map/ppermute | solution.py:195
  41.3 1.9 %collective-permute-start.4 = (bf16[16,4096]{1,0:T(8,128)(2,1)S(1)}, bf16[16,4096]{1,0:T(8,128)(2,1)S(1)}, u32[]{:S(2)}, u32[]{:S(2)}) collective-permute-start(bf16[16,4096]{1,0:T(8,128)(2,1)S(1)} %get-tuple-element.22), channel_id=1, source_target_pairs={{0,1},{1,0},{2,3},{3,2},{4,5},{5,4},{6,7},{7,6},{8,9},{9,8},{10,11... | collective-permute-start | bytes 393224 | tf_op jit(solution)/shard_map/ppermute | solution.py:195
  43.2 0.0 collective-permute-done.2
  43.2 2.4 %collective-permute-done.3 = bf16[16,4096]{1,0:T(8,128)(2,1)S(1)} collective-permute-done((bf16[16,4096]{1,0:T(8,128)(2,1)S(1)}, bf16[16,4096]{1,0:T(8,128)(2,1)S(1)}, u32[]{:S(2)}, u32[]{:S(2)}) %collective-permute-start.3) | collective-permute-done | bytes 131104 | tf_op jit(solution)/shard_map/ppermute | solution.py:195
  45.6 0.0 collective-permute-done.4
  45.6 0.8 %add_bitcast_fusion = f32[1,16,4096]{2,1,0:T(8,128)} fusion(bf16[16,4096]{1,0:T(8,128)(2,1)S(1)} %collective-permute-done.4, bf16[16,4096]{1,0:T(8,128)(2,1)S(1)} %collective-permute-done.3, f32[16,4096]{1,0:T(8,128)S(1)} %get-tuple-element.19, bf16[16,4096]{1,0:T(8,128)(2,1)S(1)} %collective-permute-done.2), kind=kLoop, calls=%fused_computation | loop fusion | flops 393216 | bytes 917504 | tf_op jit(solution)/shard_map/broadcast_in_dim | solution.py:228
Async XLA Ops:
  0.0 32.0 %collective-permute-start.1 = (bf16[64,4096]{1,0:T(8,128)(2,1)}, bf16[64,4096]{1,0:T(8,128)(2,1)S(1)}, u32[]{:S(2)}, u32[]{:S(2)}) collective-permute-start(bf16[64,4096]{1,0:T(8,128)(2,1)} %bitcast.5), channel_id=1, source_target_pairs={{0,764},{4,0},{8,4},{12,8},{16,12},{20,16},{24,20},{28,24},{32,28}... | collective-permute-start | bytes 1572872 | tf_op jit(solution)/shard_map/ppermute | solution.py:191
  21.1 1.2 %copy-start = (s32[64,4096]{1,0:T(8,128)S(1)}, s32[64,4096]{1,0:T(8,128)}, u32[]{:S(2)}) copy-start(s32[64,4096]{1,0:T(8,128)} %mask.1) | copy-start | bytes 3145732
  22.4 1.0 %copy-start.1 = (bf16[1,64,4096]{2,1,0:T(8,128)(2,1)S(1)}, bf16[1,64,4096]{2,1,0:T(8,128)(2,1)}, u32[]{:S(2)}) copy-start(bf16[1,64,4096]{2,1,0:T(8,128)(2,1)} %param.5) | copy-start | bytes 1572868
  23.4 1.0 %copy-start.2 = (bf16[1,64,4096]{2,1,0:T(8,128)(2,1)S(1)}, bf16[1,64,4096]{2,1,0:T(8,128)(2,1)}, u32[]{:S(2)}) copy-start(bf16[1,64,4096]{2,1,0:T(8,128)(2,1)} %param.6) | copy-start | bytes 1572868
  24.4 0.9 %copy-start.3 = (bf16[512,256]{1,0:T(8,128)(2,1)S(1)}, bf16[512,256]{1,0:T(8,128)(2,1)}, u32[]{:S(2)}) copy-start(bf16[512,256]{1,0:T(8,128)(2,1)} %constant.2.clone.table) | copy-start | bytes 786436
  27.7 4.4 %collective-permute-start = (f32[8,128]{1,0:T(8,128)S(1)}, f32[8,128]{1,0:T(8,128)S(1)}, u32[]{:S(2)}, u32[]{:S(2)}) collective-permute-start(f32[8,128]{1,0:T(8,128)S(1)} %get-tuple-element.14), channel_id=1, source_target_pairs={{0,764},{4,0},{8,4},{12,8},{16,12},{20,16},{24,20},{28,24},{32,28}... | collective-permute-start | bytes 12296 | tf_op jit(solution)/shard_map/ppermute | solution.py:191
  33.7 9.5 %collective-permute-start.2 = (bf16[16,4096]{1,0:T(8,128)(2,1)S(1)}, bf16[16,4096]{1,0:T(8,128)(2,1)S(1)}, u32[]{:S(2)}, u32[]{:S(2)}) collective-permute-start(bf16[16,4096]{1,0:T(8,128)(2,1)S(1)} %get-tuple-element.20), channel_id=1, source_target_pairs={{0,2},{1,3},{2,0},{3,1},{4,6},{5,7},{6,4},{7,5},{8,10},{9,11},{10,... | collective-permute-start | bytes 393224 | tf_op jit(solution)/shard_map/ppermute | solution.py:195
  35.9 9.7 %collective-permute-start.3 = (bf16[16,4096]{1,0:T(8,128)(2,1)S(1)}, bf16[16,4096]{1,0:T(8,128)(2,1)S(1)}, u32[]{:S(2)}, u32[]{:S(2)}) collective-permute-start(bf16[16,4096]{1,0:T(8,128)(2,1)S(1)} %get-tuple-element.21), channel_id=1, source_target_pairs={{0,3},{1,2},{2,1},{3,0},{4,7},{5,6},{6,5},{7,4},{8,11},{9,10},{10,... | collective-permute-start | bytes 393224 | tf_op jit(solution)/shard_map/ppermute | solution.py:195
  41.3 4.3 %collective-permute-start.4 = (bf16[16,4096]{1,0:T(8,128)(2,1)S(1)}, bf16[16,4096]{1,0:T(8,128)(2,1)S(1)}, u32[]{:S(2)}, u32[]{:S(2)}) collective-permute-start(bf16[16,4096]{1,0:T(8,128)(2,1)S(1)} %get-tuple-element.22), channel_id=1, source_target_pairs={{0,1},{1,0},{2,3},{3,2},{4,5},{5,4},{6,7},{7,6},{8,9},{9,8},{10,11... | collective-permute-start | bytes 393224 | tf_op jit(solution)/shard_map/ppermute | solution.py:195

commit v3 on v2

--- a/solution.py
+++ b/solution.py
@@ -18,6 +18,7 @@
 CHUNK = 256
 MEMBERS = 4
 SLAB = N // MEMBERS
+PACKED = N * N + LANES
 
 DIAG, CAS, CAS_ROWS, CAS_COLS, EVEN_FIRST, TABLE_ROWS = 0, 256, 320, 384, 448, 512
 
@@ -105,20 +106,34 @@
         emit(block, potential * scale * by_owner(me, source, columns_of(block)).astype(jnp.float32))
 
 
-def own_kernel(count, label, target, source, mask, table, field, kernel, weight, target_out, table_out,
-               source_in, mask_in, turned, rows, sems):
+def on_last_band():
+    return lax.axis_index("band") == lax.axis_size("band") - 1
+
+
+def pack_kernel(label, source, packed, sem):
+    copy = pltpu.make_async_copy(source, packed.at[:, : N * N], sem)
+    copy.start()
+    for half, part in enumerate((label[0] // 8, label[0] % 8)):
+        packed[half * HALF : (half + 1) * HALF, N * N :] = (
+            jnp.full((HALF, LANES), part, jnp.int32).astype(jnp.float32).astype(jnp.bfloat16)
+        )
+    copy.wait()
+
+
+def minus_occupation(count, packed):
+    high, low = (packed[half * HALF : half * HALF + 16, N * N :].astype(jnp.float32) for half in range(2))
+    shifted = (8.0 * high + low - count / 2.0) / (count / 4.0)
+    return (-1.0 / (1.0 + jnp.exp(shifted)))[:1, :1]
+
+
+def own_body(count, target, packed, mask, table, field, kernel, target_in, table_in, mask_in, turned, rows, sems):
     copies = [
         pltpu.make_async_copy(a, b, sems.at[i])
-        for i, (a, b) in enumerate(
-            ((target, target_out), (source, source_in), (table, table_out), (mask, mask_in))
-        )
+        for i, (a, b) in enumerate(((target, target_in), (table, table_in), (mask, mask_in)))
     ]
     for copy in copies:
         copy.start()
     me = lax.axis_index("group")
-    shifted = (jnp.full((8, LANES), label[0], jnp.int32).astype(jnp.float32) - count / 2.0) / (count / 4.0)
-    scale = -1.0 / (1.0 + jnp.exp(shifted))
-    weight[...] = scale
     low = low_lanes()
     ky = lax.broadcasted_iota(jnp.int32, (N, LANES), 0)
     lane = lax.broadcasted_iota(jnp.int32, (N, LANES), 1)
@@ -128,10 +143,9 @@
         return signed * signed
 
     plane = squared(ky) + squared(lane % N)
-
     for copy in copies:
         copy.wait()
-    even_first = table_out[EVEN_FIRST:, :N]
+    even_first = table_in[EVEN_FIRST:, :N]
     for block in range(BLOCKS):
         kept = dot(even_first, mask_in[:, columns_of(block)].astype(jnp.float32).astype(jnp.bfloat16))
         for part in range(2):
@@ -147,12 +161,22 @@
     def emit(block, value):
         field[:, columns_of(block)] = value
 
-    pair_field(me, target_out, source_in, scale[:1, :1], lambda: kernel, table_out, turned, rows, emit)
-
-
-def cross_kernel(weight, target, source, field, kernel, table, mine, *rest):
-    sent, (turned, rows) = rest[: MEMBERS - 1], rest[MEMBERS - 1 :]
-
+    pair_field(me, target_in, packed, minus_occupation(count, packed), lambda: kernel, table_in, turned, rows, emit)
+
+
+def own_kernel(count, *refs):
+    @pl.when(jnp.logical_not(on_last_band()))
+    def _():
+        own_body(count, *refs)
+
+
+def own_last_kernel(count, *refs):
+    @pl.when(on_last_band())
+    def _():
+        own_body(count, *refs)
+
+
+def cross_body(count, target, packed, field, kernel, table, mine, sent, scratch):
     def emit(block, value):
         total = field[:, columns_of(block)] + value
         mine[:, columns_of(block)] = total[:SLAB]
@@ -160,8 +184,24 @@
             sent[k - 1][:, columns_of(block)] = total[k * SLAB : (k + 1) * SLAB].astype(jnp.bfloat16)
 
     pair_field(
-        lax.axis_index("group"), target, source, weight[:1, :1], lambda: kernel, table, turned, rows, emit
-    )
+        lax.axis_index("group"), target, packed, minus_occupation(count, packed), lambda: kernel, table, *scratch, emit
+    )
+
+
+def cross_kernel(count, target, packed, field, kernel, table, mine, *rest):
+    @pl.when(jnp.logical_not(on_last_band()))
+    def _():
+        cross_body(count, target, packed, field, kernel, table, mine, rest[: MEMBERS - 1], rest[MEMBERS - 1 :])
+
+
+def cross_last_kernel(count, target, packed, field, kernel, table, held, mine, *rest):
+    @pl.when(on_last_band())
+    def _():
+        cross_body(count, target, packed, field, kernel, table, mine, rest[: MEMBERS - 1], rest[MEMBERS - 1 :])
+
+    @pl.when(jnp.logical_not(on_last_band()))
+    def _():
+        mine[...] = held[...]
 
 
 def shape(rows, columns, dtype):
@@ -169,62 +209,80 @@
 
 
 PAIR_SCRATCH = [pltpu.VMEM((HALF * STRIDE, LANES), jnp.float32), pltpu.VMEM((BLOCKS * N, WIDE), jnp.bfloat16)]
+OWN_SCRATCH = [pltpu.VMEM((N, N * N), jnp.int32)] + PAIR_SCRATCH + [pltpu.SemaphoreType.DMA((3,))]
 VMEM = pl.BlockSpec(memory_space=pltpu.VMEM)
 HBM = pl.BlockSpec(memory_space=pltpu.HBM)
 
 
-def call(kernel, outs, in_specs, scratch, name):
+def call(kernel, outs, in_specs, scratch, name, aliases=None, flops=6 * 2 * N**4):
     return pl.pallas_call(
         kernel,
         out_shape=outs,
         in_specs=in_specs,
         out_specs=[VMEM] * len(outs),
         scratch_shapes=scratch,
+        input_output_aliases=aliases or {},
         compiler_params=pltpu.CompilerParams(vmem_limit_bytes=40 * 1024 * 1024),
-        cost_estimate=pl.CostEstimate(flops=6 * 2 * N**4, bytes_accessed=4 * 1024 * 1024, transcendentals=0),
+        cost_estimate=pl.CostEstimate(flops=flops, bytes_accessed=4 * 1024 * 1024, transcendentals=0),
         name=name,
     )
 
 
-def passed_along(value, axis, steps):
-    count = lax.axis_size(axis)
-    return lax.ppermute(value, axis, [(s, (s + steps) % count) for s in range(count)])
-
-
-def swapped(value, bits):
-    return lax.ppermute(value, "group", [(s, s ^ bits) for s in range(MEMBERS)])
+def in_hbm(value):
+    return pltpu.with_memory_space_constraint(value, pltpu.HBM)
+
+
+def sent_along(value, pairs):
+    return lax.ppermute(value, ("band", "group"), [(s[0] * MEMBERS + s[1], t[0] * MEMBERS + t[1]) for s, t in pairs])
+
+
+def exchanged(sent, bands):
+    return [
+        sent_along(sent[bits - 1], [((b, g), (b, g ^ bits)) for b in bands for g in range(MEMBERS)]) for bits in (2, 3, 1)
+    ]
 
 
 def shards(trial, orbitals, labels, kernel_mask):
-    count = lax.axis_size("band") * lax.axis_size("group")
-    target, source = trial[0], orbitals[0]
-    next_source = passed_along(source, "band", -1)
-    field, kernel, weight, target, table = call(
-        functools.partial(own_kernel, count),
-        (
-            shape(N, N * N, jnp.float32),
-            shape(BLOCKS * N, WIDE, jnp.float32),
-            shape(8, LANES, jnp.float32),
-            shape(N, N * N, jnp.bfloat16),
-            shape(TABLE_ROWS, WIDE, jnp.bfloat16),
-        ),
-        [pl.BlockSpec(memory_space=pltpu.SMEM)] + [HBM] * 4,
-        [pltpu.VMEM((N, N * N), jnp.bfloat16), pltpu.VMEM((N, N * N), jnp.int32)]
-        + PAIR_SCRATCH
-        + [pltpu.SemaphoreType.DMA((4,))],
-        "own",
-    )(labels, target, source, kernel_mask, tables())
-    next_weight = passed_along(weight, "band", -1)
+    bands = lax.axis_size("band")
+    count = bands * MEMBERS
+    last = bands - 1
+    members = range(MEMBERS)
+    target, table, mask = in_hbm(trial[0]), in_hbm(tables()), in_hbm(kernel_mask)
+    packed = call(
+        pack_kernel,
+        [shape(N, PACKED, jnp.bfloat16)],
+        [pl.BlockSpec(memory_space=pltpu.SMEM), HBM],
+        [pltpu.SemaphoreType.DMA],
+        "pack",
+        flops=0,
+    )(labels, in_hbm(orbitals[0]))[0]
+    following = sent_along(packed, [((b, g), (b - 1, g)) for b in range(1, bands) for g in members])
+    planes = [
+        shape(N, N * N, jnp.float32),
+        shape(BLOCKS * N, WIDE, jnp.float32),
+        shape(N, N * N, jnp.bfloat16),
+        shape(TABLE_ROWS, WIDE, jnp.bfloat16),
+    ]
+    sources = [HBM, VMEM, HBM, HBM]
+    field, kernel, kept_target, kept_table = call(
+        functools.partial(own_kernel, count), planes, sources, OWN_SCRATCH, "own"
+    )(target, packed, mask, table)
+    packed, field = lax.optimization_barrier((packed, field))
+    wrapped = sent_along(packed, [((0, g), (last, g)) for g in members])
+    last_field, last_kernel, last_target, last_table = call(
+        functools.partial(own_last_kernel, count), planes, sources, OWN_SCRATCH, "own_last"
+    )(target, packed, mask, table)
+    slabs = [shape(SLAB, N * N, jnp.float32)] + [shape(SLAB, N * N, jnp.bfloat16)] * (MEMBERS - 1)
+    mine, *sent = call(functools.partial(cross_kernel, count), slabs, [VMEM] * 5, PAIR_SCRATCH, "cross")(
+        kept_target, following, field, kernel, kept_table
+    )
+    received = exchanged(sent, range(last))
+    wrapped, *received = lax.optimization_barrier((wrapped, *received))
     mine, *sent = call(
-        cross_kernel,
-        [shape(SLAB, N * N, jnp.float32)] + [shape(SLAB, N * N, jnp.bfloat16)] * (MEMBERS - 1),
-        [VMEM] * 6,
-        PAIR_SCRATCH,
-        "cross",
-    )(next_weight, target, next_source, field, kernel, table)
-    received = {bits: swapped(sent[bits - 1], bits) for bits in (2, 3, 1)}
-    for bits in (2, 3, 1):
-        mine = mine + received[bits].astype(jnp.float32)
+        functools.partial(cross_last_kernel, count), slabs, [VMEM] * 6, PAIR_SCRATCH, "cross_last", aliases={5: 0}
+    )(last_target, wrapped, last_field, last_kernel, last_table, mine)
+    for piece in received + exchanged(sent, [last]):
+        mine = mine + piece.astype(jnp.float32)
     return mine[None]
 
 

time: 46.8 us -> 41.3 us (0.88)
  local copies, waits for them, and re-layouts: 4.25 us -> 0 us
  Pallas kernels: 3.96 us -> 6.35 us
  starting transfers between devices: 32.9 us -> 30.7 us
  waiting for transfers between devices: 3.77 us -> 2.34 us
    unnamed x8 -> x0, local copies, waits for them, and re-layouts: 4.25 us -> none
    pallas_call x2 -> x5, Pallas kernels: 3.96 us -> 6.35 us  [the longest x1 3.54 us: shards(): call(functools.partial(own_kernel, count), planes, sources, OWN_SCRATCH,...]
    ppermute x5 -> x8, starting transfers between devices: 32.9 us -> 30.7 us  [sent_along(): lax.ppermute(value, ('band', 'group'), [(s[0] * MEMBERS + s[1], t[0] * ME...]
    ppermute x5 -> x8, waiting for transfers between devices: 3.77 us -> 2.34 us  [sent_along(): lax.ppermute(value, ('band', 'group'), [(s[0] * MEMBERS + s[1], t[0] * ME...]
  transfers between devices with their start and end apart: 5 -> 8, of which waited for: 2 -> 2; matrix products, arithmetic and copies ran while one was open for 0% -> 0% of each run, Pallas kernels for 5% -> 13%
where the time goes in v3:
time: 41.3 us; the launch traced here: 40.9 us
  starting transfers between devices  30.7 us (74%)
  Pallas kernels  6.35 us (15%)
  waiting for transfers between devices  2.34 us (6%)
  other arithmetic  0.81 us (2%)
  between operations  0.79 us (2%)
    ppermute x8, starting transfers between devices, sent_along(): lax.ppermute(value, ('band', 'group'), [(s[0] * MEMBERS + s[1], t[0] * ME...  30.7 us
    pallas_call x1, Pallas kernels, shards(): call(functools.partial(own_kernel, count), planes, sources, OWN_SCRATCH,...  3.54 us
    ppermute x8, waiting for transfers between devices, sent_along(): lax.ppermute(value, ('band', 'group'), [(s[0] * MEMBERS + s[1], t[0] * ME...  2.34 us
    pallas_call x1, Pallas kernels, shards(): call(functools.partial(cross_kernel, count), slabs, [VMEM] * 5, PAIR_SCRA...  1.67 us
    pallas_call x1, Pallas kernels, shards(): call(pack_kernel, [shape(N, PACKED, jnp.bfloat16)], [pl.BlockSpec(memory_...  1.05 us
  transfers between devices with their start and end apart: 8, of which 2 were waited for; matrix products, arithmetic and copies ran while one was open for 0% of the time, Pallas kernels for 13%

profile of v3, /device:TPU:1, one launch (start us, length us, event | category | flops | bytes accessed | tf_op | source)
XLA Modules:
  0.0 40.9 jit_solution(4011431808552448672)
XLA Ops:
  0.7 1.1 %pack.1.refs_1_ = bf16[64,4224]{1,0:T(8,128)(2,1)S(1)} custom-call(s32[1]{0:T(128)S(6)} %copy.8.label, bf16[64,4096]{1,0:T(8,128)(2,1)} %bitcast.6), custom_call_target="tpu_custom_call" | custom-call | bytes 4194304 | tf_op jit(solution)/shard_map/pack/pallas_call | solution.py:251
  1.7 1.3 %collective-permute-start.1 = (bf16[64,4224]{1,0:T(8,128)(2,1)S(1)}, bf16[64,4224]{1,0:T(8,128)(2,1)S(1)}, u32[]{:S(2)}, u32[]{:S(2)}) collective-permute-start(bf16[64,4224]{1,0:T(8,128)(2,1)S(1)} %pack.1.refs_1_), channel_id=1, source_target_pairs={{4,0},{5,1},{6,2},{7,3},{8,4},{9,5},{10,6},{11,7},{12,8},{13,9},{1... | collective-permute-start | bytes 1622024 | tf_op jit(solution)/shard_map/ppermute | solution.py:236
  3.0 3.5 %own.1 = (f32[64,4096]{1,0:T(8,128)S(1)}, f32[1024,256]{1,0:T(8,128)S(1)}, bf16[64,4096]{1,0:T(8,128)(2,1)S(1)}, bf16[512,256]{1,0:T(8,128)(2,1)S(1)}) custom-call(bf16[64,4096]{1,0:T(8,128)(2,1)} %bitcast.4, bf16[64,4224]{1,0:T(8,128)(2,1)S(1)} %pack.1.refs_1_, s32[64,4096]{1,0:T(8,128)} %refs_2_.3, bf16[512,256]{1,0:T(8,128)(2,1)} %constant.2.clone.refs_3_), custom_call_target="tpu_custom_call" | custom-call | flops 201326592 | bytes 4194304 | tf_op jit(solution)/shard_map/own/pallas_call | solution.py:267
  6.6 18.7 %collective-permute-start = (bf16[64,4224]{1,0:T(8,128)(2,1)S(1)}, bf16[64,4224]{1,0:T(8,128)(2,1)S(1)}, u32[]{:S(2)}, u32[]{:S(2)}) collective-permute-start(bf16[64,4224]{1,0:T(8,128)(2,1)S(1)} %pack.1.refs_1_), channel_id=1, source_target_pairs={{0,764},{1,765},{2,766},{3,767}} | collective-permute-start | bytes 1622024 | tf_op jit(solution)/shard_map/ppermute | solution.py:236
  25.3 0.0 collective-permute-done.1.packed
  25.3 1.7 %cross.1 = (f32[16,4096]{1,0:T(8,128)S(1)}, bf16[16,4096]{1,0:T(8,128)(2,1)S(1)}, bf16[16,4096]{1,0:T(8,128)(2,1)S(1)}, bf16[16,4096]{1,0:T(8,128)(2,1)S(1)}) custom-call(bf16[64,4096]{1,0:T(8,128)(2,1)S(1)} %get-tuple-element.30.target, bf16[64,4224]{1,0:T(8,128)(2,1)S(1)} %collective-permute-done.1.packed, f32[64,4096]{1,0:T(8,128)S(1)} %get-tuple-element.31.field, ...), custom_call_target="tpu_custom_call" | custom-call | flops 201326592 | bytes 4194304 | tf_op jit(solution)/shard_map/cross/pallas_call | solution.py:276
  27.0 2.2 %collective-permute-start.2 = (bf16[16,4096]{1,0:T(8,128)(2,1)S(1)}, bf16[16,4096]{1,0:T(8,128)(2,1)S(1)}, u32[]{:S(2)}, u32[]{:S(2)}) collective-permute-start(bf16[16,4096]{1,0:T(8,128)(2,1)S(1)} %get-tuple-element.34), channel_id=1, source_target_pairs={{0,2},{1,3},{2,0},{3,1},{4,6},{5,7},{6,4},{7,5},{8,10},{9,11},{10,... | collective-permute-start | bytes 393224 | tf_op jit(solution)/shard_map/ppermute | solution.py:236
  29.2 4.5 %collective-permute-start.3 = (bf16[16,4096]{1,0:T(8,128)(2,1)S(1)}, bf16[16,4096]{1,0:T(8,128)(2,1)S(1)}, u32[]{:S(2)}, u32[]{:S(2)}) collective-permute-start(bf16[16,4096]{1,0:T(8,128)(2,1)S(1)} %get-tuple-element.35), channel_id=1, source_target_pairs={{0,3},{1,2},{2,1},{3,0},{4,7},{5,6},{6,5},{7,4},{8,11},{9,10},{10,... | collective-permute-start | bytes 393224 | tf_op jit(solution)/shard_map/ppermute | solution.py:236
  33.7 1.9 %collective-permute-start.4 = (bf16[16,4096]{1,0:T(8,128)(2,1)S(1)}, bf16[16,4096]{1,0:T(8,128)(2,1)S(1)}, u32[]{:S(2)}, u32[]{:S(2)}) collective-permute-start(bf16[16,4096]{1,0:T(8,128)(2,1)S(1)} %get-tuple-element.36), channel_id=1, source_target_pairs={{0,1},{1,0},{2,3},{3,2},{4,5},{5,4},{6,7},{7,6},{8,9},{9,8},{10,11... | collective-permute-start | bytes 393224 | tf_op jit(solution)/shard_map/ppermute | solution.py:236
  35.6 0.1 own_last.1
  35.7 0.2 collective-permute-done.packed
  35.9 0.0 collective-permute-done.2
  35.9 2.1 %collective-permute-done.3 = bf16[16,4096]{1,0:T(8,128)(2,1)S(1)} collective-permute-done((bf16[16,4096]{1,0:T(8,128)(2,1)S(1)}, bf16[16,4096]{1,0:T(8,128)(2,1)S(1)}, u32[]{:S(2)}, u32[]{:S(2)}) %collective-permute-start.3) | collective-permute-done | bytes 131104 | tf_op jit(solution)/shard_map/ppermute | solution.py:236
  38.0 0.0 collective-permute-done.4
  38.1 0.7 %collective-permute-start.5 = (bf16[16,4096]{1,0:T(8,128)(2,1)S(1)}, bf16[16,4096]{1,0:T(8,128)(2,1)S(1)}, u32[]{:S(2)}, u32[]{:S(2)}) collective-permute-start(bf16[16,4096]{1,0:T(8,128)(2,1)S(1)} %get-tuple-element.46), channel_id=1, source_target_pairs={{764,766},{765,767},{766,764},{767,765}} | collective-permute-start | bytes 393224 | tf_op jit(solution)/shard_map/ppermute | solution.py:236
  38.7 0.7 %collective-permute-start.6 = (bf16[16,4096]{1,0:T(8,128)(2,1)S(1)}, bf16[16,4096]{1,0:T(8,128)(2,1)S(1)}, u32[]{:S(2)}, u32[]{:S(2)}) collective-permute-start(bf16[16,4096]{1,0:T(8,128)(2,1)S(1)} %get-tuple-element.47), channel_id=1, source_target_pairs={{764,767},{765,766},{766,765},{767,764}} | collective-permute-start | bytes 393224 | tf_op jit(solution)/shard_map/ppermute | solution.py:236
  39.4 0.7 %collective-permute-start.7 = (bf16[16,4096]{1,0:T(8,128)(2,1)S(1)}, bf16[16,4096]{1,0:T(8,128)(2,1)S(1)}, u32[]{:S(2)}, u32[]{:S(2)}) collective-permute-start(bf16[16,4096]{1,0:T(8,128)(2,1)S(1)} %get-tuple-element.48), channel_id=1, source_target_pairs={{764,765},{765,764},{766,767},{767,766}} | collective-permute-start | bytes 393224 | tf_op jit(solution)/shard_map/ppermute | solution.py:236
  40.1 0.0 collective-permute-done.5
  40.1 0.0 collective-permute-done.6
  40.1 0.0 collective-permute-done.7
  40.1 0.8 %add_bitcast_fusion = f32[1,16,4096]{2,1,0:T(8,128)} fusion(bf16[16,4096]{1,0:T(8,128)(2,1)S(1)} %collective-permute-done.7, bf16[16,4096]{1,0:T(8,128)(2,1)S(1)} %collective-permute-done.6, bf16[16,4096]{1,0:T(8,128)(2,1)S(1)} %collective-permute-done.5, bf16[16,4096]{1,0:T(8,128)(2,1)S(1)} %collective-permute-done.4, ...), kind=kLoop, calls=%fused_computation | loop fusion | flops 786432 | bytes 1310720 | tf_op jit(solution)/shard_map/broadcast_in_dim | solution.py:286
  (1 shorter events, 0.0 us)
Async XLA Ops:
  1.7 23.6 %collective-permute-start.1 = (bf16[64,4224]{1,0:T(8,128)(2,1)S(1)}, bf16[64,4224]{1,0:T(8,128)(2,1)S(1)}, u32[]{:S(2)}, u32[]{:S(2)}) collective-permute-start(bf16[64,4224]{1,0:T(8,128)(2,1)S(1)} %pack.1.refs_1_), channel_id=1, source_target_pairs={{4,0},{5,1},{6,2},{7,3},{8,4},{9,5},{10,6},{11,7},{12,8},{13,9},{1... | collective-permute-start | bytes 1622024 | tf_op jit(solution)/shard_map/ppermute | solution.py:236
  6.6 29.4 %collective-permute-start = (bf16[64,4224]{1,0:T(8,128)(2,1)S(1)}, bf16[64,4224]{1,0:T(8,128)(2,1)S(1)}, u32[]{:S(2)}, u32[]{:S(2)}) collective-permute-start(bf16[64,4224]{1,0:T(8,128)(2,1)S(1)} %pack.1.refs_1_), channel_id=1, source_target_pairs={{0,764},{1,765},{2,766},{3,767}} | collective-permute-start | bytes 1622024 | tf_op jit(solution)/shard_map/ppermute | solution.py:236
  27.0 8.9 %collective-permute-start.2 = (bf16[16,4096]{1,0:T(8,128)(2,1)S(1)}, bf16[16,4096]{1,0:T(8,128)(2,1)S(1)}, u32[]{:S(2)}, u32[]{:S(2)}) collective-permute-start(bf16[16,4096]{1,0:T(8,128)(2,1)S(1)} %get-tuple-element.34), channel_id=1, source_target_pairs={{0,2},{1,3},{2,0},{3,1},{4,6},{5,7},{6,4},{7,5},{8,10},{9,11},{10,... | collective-permute-start | bytes 393224 | tf_op jit(solution)/shard_map/ppermute | solution.py:236
  29.2 8.8 %collective-permute-start.3 = (bf16[16,4096]{1,0:T(8,128)(2,1)S(1)}, bf16[16,4096]{1,0:T(8,128)(2,1)S(1)}, u32[]{:S(2)}, u32[]{:S(2)}) collective-permute-start(bf16[16,4096]{1,0:T(8,128)(2,1)S(1)} %get-tuple-element.35), channel_id=1, source_target_pairs={{0,3},{1,2},{2,1},{3,0},{4,7},{5,6},{6,5},{7,4},{8,11},{9,10},{10,... | collective-permute-start | bytes 393224 | tf_op jit(solution)/shard_map/ppermute | solution.py:236
  33.7 4.3 %collective-permute-start.4 = (bf16[16,4096]{1,0:T(8,128)(2,1)S(1)}, bf16[16,4096]{1,0:T(8,128)(2,1)S(1)}, u32[]{:S(2)}, u32[]{:S(2)}) collective-permute-start(bf16[16,4096]{1,0:T(8,128)(2,1)S(1)} %get-tuple-element.36), channel_id=1, source_target_pairs={{0,1},{1,0},{2,3},{3,2},{4,5},{5,4},{6,7},{7,6},{8,9},{9,8},{10,11... | collective-permute-start | bytes 393224 | tf_op jit(solution)/shard_map/ppermute | solution.py:236
  38.1 2.0 %collective-permute-start.5 = (bf16[16,4096]{1,0:T(8,128)(2,1)S(1)}, bf16[16,4096]{1,0:T(8,128)(2,1)S(1)}, u32[]{:S(2)}, u32[]{:S(2)}) collective-permute-start(bf16[16,4096]{1,0:T(8,128)(2,1)S(1)} %get-tuple-element.46), channel_id=1, source_target_pairs={{764,766},{765,767},{766,764},{767,765}} | collective-permute-start | bytes 393224 | tf_op jit(solution)/shard_map/ppermute | solution.py:236
  38.7 1.4 %collective-permute-start.6 = (bf16[16,4096]{1,0:T(8,128)(2,1)S(1)}, bf16[16,4096]{1,0:T(8,128)(2,1)S(1)}, u32[]{:S(2)}, u32[]{:S(2)}) collective-permute-start(bf16[16,4096]{1,0:T(8,128)(2,1)S(1)} %get-tuple-element.47), channel_id=1, source_target_pairs={{764,767},{765,766},{766,765},{767,764}} | collective-permute-start | bytes 393224 | tf_op jit(solution)/shard_map/ppermute | solution.py:236
  39.4 0.7 %collective-permute-start.7 = (bf16[16,4096]{1,0:T(8,128)(2,1)S(1)}, bf16[16,4096]{1,0:T(8,128)(2,1)S(1)}, u32[]{:S(2)}, u32[]{:S(2)}) collective-permute-start(bf16[16,4096]{1,0:T(8,128)(2,1)S(1)} %get-tuple-element.48), channel_id=1, source_target_pairs={{764,765},{765,764},{766,767},{767,766}} | collective-permute-start | bytes 393224 | tf_op jit(solution)/shard_map/ppermute | solution.py:236

commit v4 on v3

--- a/solution.py
+++ b/solution.py
@@ -19,6 +19,8 @@
 MEMBERS = 4
 SLAB = N // MEMBERS
 PACKED = N * N + LANES
+PACK_COPIES = 4
+LATE = 2
 
 DIAG, CAS, CAS_ROWS, CAS_COLS, EVEN_FIRST, TABLE_ROWS = 0, 256, 320, 384, 448, 512
 
@@ -106,18 +108,26 @@
         emit(block, potential * scale * by_owner(me, source, columns_of(block)).astype(jnp.float32))
 
 
-def on_last_band():
-    return lax.axis_index("band") == lax.axis_size("band") - 1
-
-
-def pack_kernel(label, source, packed, sem):
-    copy = pltpu.make_async_copy(source, packed.at[:, : N * N], sem)
-    copy.start()
+def on_late_band():
+    return lax.axis_index("band") >= lax.axis_size("band") - LATE
+
+
+def pack_kernel(label, source, packed, sems):
+    step = N * N // PACK_COPIES
+    copies = [
+        pltpu.make_async_copy(
+            source.at[:, i * step : (i + 1) * step], packed.at[:, i * step : (i + 1) * step], sems.at[i]
+        )
+        for i in range(PACK_COPIES)
+    ]
+    for copy in copies:
+        copy.start()
     for half, part in enumerate((label[0] // 8, label[0] % 8)):
         packed[half * HALF : (half + 1) * HALF, N * N :] = (
             jnp.full((HALF, LANES), part, jnp.int32).astype(jnp.float32).astype(jnp.bfloat16)
         )
-    copy.wait()
+    for copy in copies:
+        copy.wait()
 
 
 def minus_occupation(count, packed):
@@ -165,13 +175,13 @@
 
 
 def own_kernel(count, *refs):
-    @pl.when(jnp.logical_not(on_last_band()))
+    @pl.when(jnp.logical_not(on_late_band()))
     def _():
         own_body(count, *refs)
 
 
-def own_last_kernel(count, *refs):
-    @pl.when(on_last_band())
+def own_late_kernel(count, *refs):
+    @pl.when(on_late_band())
     def _():
         own_body(count, *refs)
 
@@ -189,17 +199,17 @@
 
 
 def cross_kernel(count, target, packed, field, kernel, table, mine, *rest):
-    @pl.when(jnp.logical_not(on_last_band()))
+    @pl.when(jnp.logical_not(on_late_band()))
     def _():
         cross_body(count, target, packed, field, kernel, table, mine, rest[: MEMBERS - 1], rest[MEMBERS - 1 :])
 
 
-def cross_last_kernel(count, target, packed, field, kernel, table, held, mine, *rest):
-    @pl.when(on_last_band())
+def cross_late_kernel(count, target, packed, field, kernel, table, held, mine, *rest):
+    @pl.when(on_late_band())
     def _():
         cross_body(count, target, packed, field, kernel, table, mine, rest[: MEMBERS - 1], rest[MEMBERS - 1 :])
 
-    @pl.when(jnp.logical_not(on_last_band()))
+    @pl.when(jnp.logical_not(on_late_band()))
     def _():
         mine[...] = held[...]
 
@@ -252,11 +262,11 @@
         pack_kernel,
         [shape(N, PACKED, jnp.bfloat16)],
         [pl.BlockSpec(memory_space=pltpu.SMEM), HBM],
-        [pltpu.SemaphoreType.DMA],
+        [pltpu.SemaphoreType.DMA((PACK_COPIES,))],
         "pack",
         flops=0,
     )(labels, in_hbm(orbitals[0]))[0]
-    following = sent_along(packed, [((b, g), (b - 1, g)) for b in range(1, bands) for g in members])
+    following = sent_along(packed, [((b, g), (b - 1, g)) for b in range(1, last) for g in members])
     planes = [
         shape(N, N * N, jnp.float32),
         shape(BLOCKS * N, WIDE, jnp.float32),
@@ -268,20 +278,19 @@
         functools.partial(own_kernel, count), planes, sources, OWN_SCRATCH, "own"
     )(target, packed, mask, table)
     packed, field = lax.optimization_barrier((packed, field))
-    wrapped = sent_along(packed, [((0, g), (last, g)) for g in members])
-    last_field, last_kernel, last_target, last_table = call(
-        functools.partial(own_last_kernel, count), planes, sources, OWN_SCRATCH, "own_last"
+    wrapped = sent_along(packed, [((s, g), (t, g)) for s, t in ((0, last), (last, last - 1)) for g in members])
+    late_field, late_kernel, late_target, late_table = call(
+        functools.partial(own_late_kernel, count), planes, sources, OWN_SCRATCH, "own_late"
     )(target, packed, mask, table)
     slabs = [shape(SLAB, N * N, jnp.float32)] + [shape(SLAB, N * N, jnp.bfloat16)] * (MEMBERS - 1)
     mine, *sent = call(functools.partial(cross_kernel, count), slabs, [VMEM] * 5, PAIR_SCRATCH, "cross")(
         kept_target, following, field, kernel, kept_table
     )
-    received = exchanged(sent, range(last))
-    wrapped, *received = lax.optimization_barrier((wrapped, *received))
+    received = exchanged(sent, range(bands - LATE))
     mine, *sent = call(
-        functools.partial(cross_last_kernel, count), slabs, [VMEM] * 6, PAIR_SCRATCH, "cross_last", aliases={5: 0}
-    )(last_target, wrapped, last_field, last_kernel, last_table, mine)
-    for piece in received + exchanged(sent, [last]):
+        functools.partial(cross_late_kernel, count), slabs, [VMEM] * 6, PAIR_SCRATCH, "cross_late", aliases={5: 0}
+    )(late_target, wrapped, late_field, late_kernel, late_table, mine)
+    for piece in received + exchanged(sent, range(bands - LATE, bands)):
         mine = mine + piece.astype(jnp.float32)
     return mine[None]
 

time: 41.3 us -> 37.2 us (0.901)
  starting transfers between devices: 30.7 us -> 28.1 us
  waiting for transfers between devices: 2.34 us -> 0.81 us
    ppermute x8, starting transfers between devices: 30.7 us -> 28.1 us  [sent_along(): lax.ppermute(value, ('band', 'group'), [(s[0] * MEMBERS + s[1], t[0] * ME...]
    ppermute x8, waiting for transfers between devices: 2.34 us -> 0.81 us  [sent_along(): lax.ppermute(value, ('band', 'group'), [(s[0] * MEMBERS + s[1], t[0] * ME...]
  transfers between devices with their start and end apart: 8 -> 8, of which waited for: 2 -> 1; matrix products, arithmetic and copies ran while one was open for 0% -> 0% of each run, Pallas kernels for 13% -> 14%
where the time goes in v4:
time: 37.2 us; the launch traced here: 36.9 us
  starting transfers between devices  28.1 us (76%)
  Pallas kernels  6.42 us (17%)
  waiting for transfers between devices  0.81 us (2%)
  other arithmetic  0.81 us (2%)
  between operations  0.81 us (2%)
    ppermute x8, starting transfers between devices, sent_along(): lax.ppermute(value, ('band', 'group'), [(s[0] * MEMBERS + s[1], t[0] * ME...  28.1 us
    pallas_call x1, Pallas kernels, shards(): call(functools.partial(own_kernel, count), planes, sources, OWN_SCRATCH,...  3.54 us
    pallas_call x1, Pallas kernels, shards(): call(functools.partial(cross_kernel, count), slabs, [VMEM] * 5, PAIR_SCRA...  1.67 us
    pallas_call x1, Pallas kernels, shards(): call(pack_kernel, [shape(N, PACKED, jnp.bfloat16)], [pl.BlockSpec(memory_...  1.13 us
    ppermute x8, waiting for transfers between devices, sent_along(): lax.ppermute(value, ('band', 'group'), [(s[0] * MEMBERS + s[1], t[0] * ME...  0.81 us
    broadcast_in_dim x1, other arithmetic, shards(): return mine[None]  0.81 us
  transfers between devices with their start and end apart: 8, of which 1 were waited for; matrix products, arithmetic and copies ran while one was open for 0% of the time, Pallas kernels for 14%

profile of v4, /device:TPU:1, one launch (start us, length us, event | category | flops | bytes accessed | tf_op | source)
XLA Modules:
  0.0 36.9 jit_solution(17626413761590608327)
XLA Ops:
  0.7 1.1 %pack.1.refs_1_ = bf16[64,4224]{1,0:T(8,128)(2,1)S(1)} custom-call(s32[1]{0:T(128)S(6)} %copy.8.label, bf16[64,4096]{1,0:T(8,128)(2,1)} %bitcast.6), custom_call_target="tpu_custom_call" | custom-call | bytes 4194304 | tf_op jit(solution)/shard_map/pack/pallas_call | solution.py:261
  1.8 1.3 %collective-permute-start.1 = (bf16[64,4224]{1,0:T(8,128)(2,1)S(1)}, bf16[64,4224]{1,0:T(8,128)(2,1)S(1)}, u32[]{:S(2)}, u32[]{:S(2)}) collective-permute-start(bf16[64,4224]{1,0:T(8,128)(2,1)S(1)} %pack.1.refs_1_), channel_id=1, source_target_pairs={{4,0},{5,1},{6,2},{7,3},{8,4},{9,5},{10,6},{11,7},{12,8},{13,9},{1... | collective-permute-start | bytes 1622024 | tf_op jit(solution)/shard_map/ppermute | solution.py:246
  3.1 3.5 %own.1 = (f32[64,4096]{1,0:T(8,128)S(1)}, f32[1024,256]{1,0:T(8,128)S(1)}, bf16[64,4096]{1,0:T(8,128)(2,1)S(1)}, bf16[512,256]{1,0:T(8,128)(2,1)S(1)}) custom-call(bf16[64,4096]{1,0:T(8,128)(2,1)} %bitcast.4, bf16[64,4224]{1,0:T(8,128)(2,1)S(1)} %pack.1.refs_1_, s32[64,4096]{1,0:T(8,128)} %refs_2_.3, bf16[512,256]{1,0:T(8,128)(2,1)} %constant.2.clone.refs_3_), custom_call_target="tpu_custom_call" | custom-call | flops 201326592 | bytes 4194304 | tf_op jit(solution)/shard_map/own/pallas_call | solution.py:277
  6.6 16.4 %collective-permute-start = (bf16[64,4224]{1,0:T(8,128)(2,1)S(1)}, bf16[64,4224]{1,0:T(8,128)(2,1)S(1)}, u32[]{:S(2)}, u32[]{:S(2)}) collective-permute-start(bf16[64,4224]{1,0:T(8,128)(2,1)S(1)} %pack.1.refs_1_), channel_id=1, source_target_pairs={{0,764},{1,765},{2,766},{3,767},{764,760},{765,761},{766,762},{767... | collective-permute-start | bytes 1622024 | tf_op jit(solution)/shard_map/ppermute | solution.py:246
  23.1 0.0 collective-permute-done.1.packed
  23.1 1.7 %cross.1 = (f32[16,4096]{1,0:T(8,128)S(1)}, bf16[16,4096]{1,0:T(8,128)(2,1)S(1)}, bf16[16,4096]{1,0:T(8,128)(2,1)S(1)}, bf16[16,4096]{1,0:T(8,128)(2,1)S(1)}) custom-call(bf16[64,4096]{1,0:T(8,128)(2,1)S(1)} %get-tuple-element.29.target, bf16[64,4224]{1,0:T(8,128)(2,1)S(1)} %collective-permute-done.1.packed, f32[64,4096]{1,0:T(8,128)S(1)} %get-tuple-element.30.field, ...), custom_call_target="tpu_custom_call" | custom-call | flops 201326592 | bytes 4194304 | tf_op jit(solution)/shard_map/cross/pallas_call | solution.py:286
  24.8 2.2 %collective-permute-start.2 = (bf16[16,4096]{1,0:T(8,128)(2,1)S(1)}, bf16[16,4096]{1,0:T(8,128)(2,1)S(1)}, u32[]{:S(2)}, u32[]{:S(2)}) collective-permute-start(bf16[16,4096]{1,0:T(8,128)(2,1)S(1)} %get-tuple-element.35), channel_id=1, source_target_pairs={{0,2},{1,3},{2,0},{3,1},{4,6},{5,7},{6,4},{7,5},{8,10},{9,11},{10,... | collective-permute-start | bytes 393224 | tf_op jit(solution)/shard_map/ppermute | solution.py:246
  27.0 0.1 own_late.1
  27.1 4.2 %collective-permute-start.3 = (bf16[16,4096]{1,0:T(8,128)(2,1)S(1)}, bf16[16,4096]{1,0:T(8,128)(2,1)S(1)}, u32[]{:S(2)}, u32[]{:S(2)}) collective-permute-start(bf16[16,4096]{1,0:T(8,128)(2,1)S(1)} %get-tuple-element.36), channel_id=1, source_target_pairs={{0,3},{1,2},{2,1},{3,0},{4,7},{5,6},{6,5},{7,4},{8,11},{9,10},{10,... | collective-permute-start | bytes 393224 | tf_op jit(solution)/shard_map/ppermute | solution.py:246
  31.3 1.9 %collective-permute-start.4 = (bf16[16,4096]{1,0:T(8,128)(2,1)S(1)}, bf16[16,4096]{1,0:T(8,128)(2,1)S(1)}, u32[]{:S(2)}, u32[]{:S(2)}) collective-permute-start(bf16[16,4096]{1,0:T(8,128)(2,1)S(1)} %get-tuple-element.37), channel_id=1, source_target_pairs={{0,1},{1,0},{2,3},{3,2},{4,5},{5,4},{6,7},{7,6},{8,9},{9,8},{10,11... | collective-permute-start | bytes 393224 | tf_op jit(solution)/shard_map/ppermute | solution.py:246
  33.2 0.8 %collective-permute-done.packed = bf16[64,4224]{1,0:T(8,128)(2,1)S(1)} collective-permute-done((bf16[64,4224]{1,0:T(8,128)(2,1)S(1)}, bf16[64,4224]{1,0:T(8,128)(2,1)S(1)}, u32[]{:S(2)}, u32[]{:S(2)}) %collective-permute-start) | collective-permute-done | bytes 540704 | tf_op jit(solution)/shard_map/ppermute | solution.py:246
  34.0 0.7 %collective-permute-start.5 = (bf16[16,4096]{1,0:T(8,128)(2,1)S(1)}, bf16[16,4096]{1,0:T(8,128)(2,1)S(1)}, u32[]{:S(2)}, u32[]{:S(2)}) collective-permute-start(bf16[16,4096]{1,0:T(8,128)(2,1)S(1)} %get-tuple-element.38), channel_id=1, source_target_pairs={{760,762},{761,763},{762,760},{763,761},{764,766},{765,767},{766,7... | collective-permute-start | bytes 393224 | tf_op jit(solution)/shard_map/ppermute | solution.py:246
  34.7 0.7 %collective-permute-start.6 = (bf16[16,4096]{1,0:T(8,128)(2,1)S(1)}, bf16[16,4096]{1,0:T(8,128)(2,1)S(1)}, u32[]{:S(2)}, u32[]{:S(2)}) collective-permute-start(bf16[16,4096]{1,0:T(8,128)(2,1)S(1)} %get-tuple-element.39), channel_id=1, source_target_pairs={{760,763},{761,762},{762,761},{763,760},{764,767},{765,766},{766,7... | collective-permute-start | bytes 393224 | tf_op jit(solution)/shard_map/ppermute | solution.py:246
  35.4 0.0 collective-permute-done.2
  35.4 0.7 %collective-permute-start.7 = (bf16[16,4096]{1,0:T(8,128)(2,1)S(1)}, bf16[16,4096]{1,0:T(8,128)(2,1)S(1)}, u32[]{:S(2)}, u32[]{:S(2)}) collective-permute-start(bf16[16,4096]{1,0:T(8,128)(2,1)S(1)} %get-tuple-element.40), channel_id=1, source_target_pairs={{760,761},{761,760},{762,763},{763,762},{764,765},{765,764},{766,7... | collective-permute-start | bytes 393224 | tf_op jit(solution)/shard_map/ppermute | solution.py:246
  36.1 0.0 collective-permute-done.3
  36.1 0.0 collective-permute-done.4
  36.1 0.0 collective-permute-done.5
  36.1 0.0 collective-permute-done.6
  36.1 0.0 collective-permute-done.7
  36.1 0.8 %add_bitcast_fusion = f32[1,16,4096]{2,1,0:T(8,128)} fusion(bf16[16,4096]{1,0:T(8,128)(2,1)S(1)} %collective-permute-done.7, bf16[16,4096]{1,0:T(8,128)(2,1)S(1)} %collective-permute-done.6, bf16[16,4096]{1,0:T(8,128)(2,1)S(1)} %collective-permute-done.5, bf16[16,4096]{1,0:T(8,128)(2,1)S(1)} %collective-permute-done.4, ...), kind=kLoop, calls=%fused_computation | loop fusion | flops 786432 | bytes 1310720 | tf_op jit(solution)/shard_map/broadcast_in_dim | solution.py:295
  (1 shorter events, 0.0 us)
Async XLA Ops:
  1.8 21.3 %collective-permute-start.1 = (bf16[64,4224]{1,0:T(8,128)(2,1)S(1)}, bf16[64,4224]{1,0:T(8,128)(2,1)S(1)}, u32[]{:S(2)}, u32[]{:S(2)}) collective-permute-start(bf16[64,4224]{1,0:T(8,128)(2,1)S(1)} %pack.1.refs_1_), channel_id=1, source_target_pairs={{4,0},{5,1},{6,2},{7,3},{8,4},{9,5},{10,6},{11,7},{12,8},{13,9},{1... | collective-permute-start | bytes 1622024 | tf_op jit(solution)/shard_map/ppermute | solution.py:246
  6.6 27.4 %collective-permute-start = (bf16[64,4224]{1,0:T(8,128)(2,1)S(1)}, bf16[64,4224]{1,0:T(8,128)(2,1)S(1)}, u32[]{:S(2)}, u32[]{:S(2)}) collective-permute-start(bf16[64,4224]{1,0:T(8,128)(2,1)S(1)} %pack.1.refs_1_), channel_id=1, source_target_pairs={{0,764},{1,765},{2,766},{3,767},{764,760},{765,761},{766,762},{767... | collective-permute-start | bytes 1622024 | tf_op jit(solution)/shard_map/ppermute | solution.py:246
  24.8 10.6 %collective-permute-start.2 = (bf16[16,4096]{1,0:T(8,128)(2,1)S(1)}, bf16[16,4096]{1,0:T(8,128)(2,1)S(1)}, u32[]{:S(2)}, u32[]{:S(2)}) collective-permute-start(bf16[16,4096]{1,0:T(8,128)(2,1)S(1)} %get-tuple-element.35), channel_id=1, source_target_pairs={{0,2},{1,3},{2,0},{3,1},{4,6},{5,7},{6,4},{7,5},{8,10},{9,11},{10,... | collective-permute-start | bytes 393224 | tf_op jit(solution)/shard_map/ppermute | solution.py:246
  27.1 9.0 %collective-permute-start.3 = (bf16[16,4096]{1,0:T(8,128)(2,1)S(1)}, bf16[16,4096]{1,0:T(8,128)(2,1)S(1)}, u32[]{:S(2)}, u32[]{:S(2)}) collective-permute-start(bf16[16,4096]{1,0:T(8,128)(2,1)S(1)} %get-tuple-element.36), channel_id=1, source_target_pairs={{0,3},{1,2},{2,1},{3,0},{4,7},{5,6},{6,5},{7,4},{8,11},{9,10},{10,... | collective-permute-start | bytes 393224 | tf_op jit(solution)/shard_map/ppermute | solution.py:246
  31.3 4.8 %collective-permute-start.4 = (bf16[16,4096]{1,0:T(8,128)(2,1)S(1)}, bf16[16,4096]{1,0:T(8,128)(2,1)S(1)}, u32[]{:S(2)}, u32[]{:S(2)}) collective-permute-start(bf16[16,4096]{1,0:T(8,128)(2,1)S(1)} %get-tuple-element.37), channel_id=1, source_target_pairs={{0,1},{1,0},{2,3},{3,2},{4,5},{5,4},{6,7},{7,6},{8,9},{9,8},{10,11... | collective-permute-start | bytes 393224 | tf_op jit(solution)/shard_map/ppermute | solution.py:246
  34.0 2.1 %collective-permute-start.5 = (bf16[16,4096]{1,0:T(8,128)(2,1)S(1)}, bf16[16,4096]{1,0:T(8,128)(2,1)S(1)}, u32[]{:S(2)}, u32[]{:S(2)}) collective-permute-start(bf16[16,4096]{1,0:T(8,128)(2,1)S(1)} %get-tuple-element.38), channel_id=1, source_target_pairs={{760,762},{761,763},{762,760},{763,761},{764,766},{765,767},{766,7... | collective-permute-start | bytes 393224 | tf_op jit(solution)/shard_map/ppermute | solution.py:246
  34.7 1.4 %collective-permute-start.6 = (bf16[16,4096]{1,0:T(8,128)(2,1)S(1)}, bf16[16,4096]{1,0:T(8,128)(2,1)S(1)}, u32[]{:S(2)}, u32[]{:S(2)}) collective-permute-start(bf16[16,4096]{1,0:T(8,128)(2,1)S(1)} %get-tuple-element.39), channel_id=1, source_target_pairs={{760,763},{761,762},{762,761},{763,760},{764,767},{765,766},{766,7... | collective-permute-start | bytes 393224 | tf_op jit(solution)/shard_map/ppermute | solution.py:246
  35.4 0.7 %collective-permute-start.7 = (bf16[16,4096]{1,0:T(8,128)(2,1)S(1)}, bf16[16,4096]{1,0:T(8,128)(2,1)S(1)}, u32[]{:S(2)}, u32[]{:S(2)}) collective-permute-start(bf16[16,4096]{1,0:T(8,128)(2,1)S(1)} %get-tuple-element.40), channel_id=1, source_target_pairs={{760,761},{761,760},{762,763},{763,762},{764,765},{765,764},{766,7... | collective-permute-start | bytes 393224 | tf_op jit(solution)/shard_map/ppermute | solution.py:246

commit v5 on v4

--- a/solution.py
+++ b/solution.py
@@ -21,6 +21,7 @@
 PACKED = N * N + LANES
 PACK_COPIES = 4
 LATE = 2
+ROW = 8
 
 DIAG, CAS, CAS_ROWS, CAS_COLS, EVEN_FIRST, TABLE_ROWS = 0, 256, 320, 384, 448, 512
 
@@ -246,6 +247,11 @@
     return lax.ppermute(value, ("band", "group"), [(s[0] * MEMBERS + s[1], t[0] * MEMBERS + t[1]) for s, t in pairs])
 
 
+def next_sources(bands):
+    count = lax.axis_size("band")
+    return [((b, g), ((b - 1) % count, g ^ 2 if b % ROW == 0 else g)) for b in bands for g in range(MEMBERS)]
+
+
 def exchanged(sent, bands):
     return [
         sent_along(sent[bits - 1], [((b, g), (b, g ^ bits)) for b in bands for g in range(MEMBERS)]) for bits in (2, 3, 1)
@@ -255,8 +261,6 @@
 def shards(trial, orbitals, labels, kernel_mask):
     bands = lax.axis_size("band")
     count = bands * MEMBERS
-    last = bands - 1
-    members = range(MEMBERS)
     target, table, mask = in_hbm(trial[0]), in_hbm(tables()), in_hbm(kernel_mask)
     packed = call(
         pack_kernel,
@@ -266,7 +270,7 @@
         "pack",
         flops=0,
     )(labels, in_hbm(orbitals[0]))[0]
-    following = sent_along(packed, [((b, g), (b - 1, g)) for b in range(1, last) for g in members])
+    following = sent_along(packed, next_sources(range(1, bands - 1)))
     planes = [
         shape(N, N * N, jnp.float32),
         shape(BLOCKS * N, WIDE, jnp.float32),
@@ -278,7 +282,7 @@
         functools.partial(own_kernel, count), planes, sources, OWN_SCRATCH, "own"
     )(target, packed, mask, table)
     packed, field = lax.optimization_barrier((packed, field))
-    wrapped = sent_along(packed, [((s, g), (t, g)) for s, t in ((0, last), (last, last - 1)) for g in members])
+    wrapped = sent_along(packed, next_sources((0, bands - 1)))
     late_field, late_kernel, late_target, late_table = call(
         functools.partial(own_late_kernel, count), planes, sources, OWN_SCRATCH, "own_late"
     )(target, packed, mask, table)

time: 37.2 us -> 37 us (level)
  no operation moved by 1% of the time
where the time goes in v5:
time: 37 us; the launch traced here: 36.7 us
  starting transfers between devices  27.8 us (75%)
  Pallas kernels  6.44 us (17%)
  waiting for transfers between devices  0.83 us (2%)
  other arithmetic  0.81 us (2%)
  between operations  0.81 us (2%)
    ppermute x8, starting transfers between devices, sent_along(): lax.ppermute(value, ('band', 'group'), [(s[0] * MEMBERS + s[1], t[0] * ME...  27.8 us
    pallas_call x1, Pallas kernels, shards(): call(functools.partial(own_kernel, count), planes, sources, OWN_SCRATCH,...  3.54 us
    pallas_call x1, Pallas kernels, shards(): call(functools.partial(cross_kernel, count), slabs, [VMEM] * 5, PAIR_SCRA...  1.68 us
    pallas_call x1, Pallas kernels, shards(): call(pack_kernel, [shape(N, PACKED, jnp.bfloat16)], [pl.BlockSpec(memory_...  1.13 us
    ppermute x8, waiting for transfers between devices, sent_along(): lax.ppermute(value, ('band', 'group'), [(s[0] * MEMBERS + s[1], t[0] * ME...  0.83 us
    broadcast_in_dim x1, other arithmetic, shards(): return mine[None]  0.81 us
  transfers between devices with their start and end apart: 8, of which 1 were waited for; matrix products, arithmetic and copies ran while one was open for 0% of the time, Pallas kernels for 14%

profile of v5, /device:TPU:1, one launch (start us, length us, event | category | flops | bytes accessed | tf_op | source)
XLA Modules:
  0.0 36.7 jit_solution(16971911597563273862)
XLA Ops:
  0.7 1.1 %pack.1.refs_1_ = bf16[64,4224]{1,0:T(8,128)(2,1)S(1)} custom-call(s32[1]{0:T(128)S(6)} %copy.8.label, bf16[64,4096]{1,0:T(8,128)(2,1)} %bitcast.6), custom_call_target="tpu_custom_call" | custom-call | bytes 4194304 | tf_op jit(solution)/shard_map/pack/pallas_call | solution.py:265
  1.8 1.3 %collective-permute-start.1 = (bf16[64,4224]{1,0:T(8,128)(2,1)S(1)}, bf16[64,4224]{1,0:T(8,128)(2,1)S(1)}, u32[]{:S(2)}, u32[]{:S(2)}) collective-permute-start(bf16[64,4224]{1,0:T(8,128)(2,1)S(1)} %pack.1.refs_1_), channel_id=1, source_target_pairs={{4,0},{5,1},{6,2},{7,3},{8,4},{9,5},{10,6},{11,7},{12,8},{13,9},{1... | collective-permute-start | bytes 1622024 | tf_op jit(solution)/shard_map/ppermute | solution.py:247
  3.1 3.5 %own.1 = (f32[64,4096]{1,0:T(8,128)S(1)}, f32[1024,256]{1,0:T(8,128)S(1)}, bf16[64,4096]{1,0:T(8,128)(2,1)S(1)}, bf16[512,256]{1,0:T(8,128)(2,1)S(1)}) custom-call(bf16[64,4096]{1,0:T(8,128)(2,1)} %bitcast.4, bf16[64,4224]{1,0:T(8,128)(2,1)S(1)} %pack.1.refs_1_, s32[64,4096]{1,0:T(8,128)} %refs_2_.3, bf16[512,256]{1,0:T(8,128)(2,1)} %constant.2.clone.refs_3_), custom_call_target="tpu_custom_call" | custom-call | flops 201326592 | bytes 4194304 | tf_op jit(solution)/shard_map/own/pallas_call | solution.py:281
  6.6 16.2 %collective-permute-start = (bf16[64,4224]{1,0:T(8,128)(2,1)S(1)}, bf16[64,4224]{1,0:T(8,128)(2,1)S(1)}, u32[]{:S(2)}, u32[]{:S(2)}) collective-permute-start(bf16[64,4224]{1,0:T(8,128)(2,1)S(1)} %pack.1.refs_1_), channel_id=1, source_target_pairs={{0,766},{1,767},{2,764},{3,765},{764,760},{765,761},{766,762},{767... | collective-permute-start | bytes 1622024 | tf_op jit(solution)/shard_map/ppermute | solution.py:247
  22.8 0.0 collective-permute-done.1.packed
  22.8 1.7 %cross.1 = (f32[16,4096]{1,0:T(8,128)S(1)}, bf16[16,4096]{1,0:T(8,128)(2,1)S(1)}, bf16[16,4096]{1,0:T(8,128)(2,1)S(1)}, bf16[16,4096]{1,0:T(8,128)(2,1)S(1)}) custom-call(bf16[64,4096]{1,0:T(8,128)(2,1)S(1)} %get-tuple-element.29.target, bf16[64,4224]{1,0:T(8,128)(2,1)S(1)} %collective-permute-done.1.packed, f32[64,4096]{1,0:T(8,128)S(1)} %get-tuple-element.30.field, ...), custom_call_target="tpu_custom_call" | custom-call | flops 201326592 | bytes 4194304 | tf_op jit(solution)/shard_map/cross/pallas_call | solution.py:290
  24.5 1.9 %collective-permute-start.2 = (bf16[16,4096]{1,0:T(8,128)(2,1)S(1)}, bf16[16,4096]{1,0:T(8,128)(2,1)S(1)}, u32[]{:S(2)}, u32[]{:S(2)}) collective-permute-start(bf16[16,4096]{1,0:T(8,128)(2,1)S(1)} %get-tuple-element.35), channel_id=1, source_target_pairs={{0,2},{1,3},{2,0},{3,1},{4,6},{5,7},{6,4},{7,5},{8,10},{9,11},{10,... | collective-permute-start | bytes 393224 | tf_op jit(solution)/shard_map/ppermute | solution.py:247
  26.4 0.1 own_late.1
  26.5 4.5 %collective-permute-start.3 = (bf16[16,4096]{1,0:T(8,128)(2,1)S(1)}, bf16[16,4096]{1,0:T(8,128)(2,1)S(1)}, u32[]{:S(2)}, u32[]{:S(2)}) collective-permute-start(bf16[16,4096]{1,0:T(8,128)(2,1)S(1)} %get-tuple-element.36), channel_id=1, source_target_pairs={{0,3},{1,2},{2,1},{3,0},{4,7},{5,6},{6,5},{7,4},{8,11},{9,10},{10,... | collective-permute-start | bytes 393224 | tf_op jit(solution)/shard_map/ppermute | solution.py:247
  31.0 1.9 %collective-permute-start.4 = (bf16[16,4096]{1,0:T(8,128)(2,1)S(1)}, bf16[16,4096]{1,0:T(8,128)(2,1)S(1)}, u32[]{:S(2)}, u32[]{:S(2)}) collective-permute-start(bf16[16,4096]{1,0:T(8,128)(2,1)S(1)} %get-tuple-element.37), channel_id=1, source_target_pairs={{0,1},{1,0},{2,3},{3,2},{4,5},{5,4},{6,7},{7,6},{8,9},{9,8},{10,11... | collective-permute-start | bytes 393224 | tf_op jit(solution)/shard_map/ppermute | solution.py:247
  32.9 0.8 %collective-permute-done.packed = bf16[64,4224]{1,0:T(8,128)(2,1)S(1)} collective-permute-done((bf16[64,4224]{1,0:T(8,128)(2,1)S(1)}, bf16[64,4224]{1,0:T(8,128)(2,1)S(1)}, u32[]{:S(2)}, u32[]{:S(2)}) %collective-permute-start) | collective-permute-done | bytes 540704 | tf_op jit(solution)/shard_map/ppermute | solution.py:247
  33.8 0.7 %collective-permute-start.5 = (bf16[16,4096]{1,0:T(8,128)(2,1)S(1)}, bf16[16,4096]{1,0:T(8,128)(2,1)S(1)}, u32[]{:S(2)}, u32[]{:S(2)}) collective-permute-start(bf16[16,4096]{1,0:T(8,128)(2,1)S(1)} %get-tuple-element.38), channel_id=1, source_target_pairs={{760,762},{761,763},{762,760},{763,761},{764,766},{765,767},{766,7... | collective-permute-start | bytes 393224 | tf_op jit(solution)/shard_map/ppermute | solution.py:247
  34.4 0.7 %collective-permute-start.6 = (bf16[16,4096]{1,0:T(8,128)(2,1)S(1)}, bf16[16,4096]{1,0:T(8,128)(2,1)S(1)}, u32[]{:S(2)}, u32[]{:S(2)}) collective-permute-start(bf16[16,4096]{1,0:T(8,128)(2,1)S(1)} %get-tuple-element.39), channel_id=1, source_target_pairs={{760,763},{761,762},{762,761},{763,760},{764,767},{765,766},{766,7... | collective-permute-start | bytes 393224 | tf_op jit(solution)/shard_map/ppermute | solution.py:247
  35.1 0.0 collective-permute-done.2
  35.1 0.7 %collective-permute-start.7 = (bf16[16,4096]{1,0:T(8,128)(2,1)S(1)}, bf16[16,4096]{1,0:T(8,128)(2,1)S(1)}, u32[]{:S(2)}, u32[]{:S(2)}) collective-permute-start(bf16[16,4096]{1,0:T(8,128)(2,1)S(1)} %get-tuple-element.40), channel_id=1, source_target_pairs={{760,761},{761,760},{762,763},{763,762},{764,765},{765,764},{766,7... | collective-permute-start | bytes 393224 | tf_op jit(solution)/shard_map/ppermute | solution.py:247
  35.8 0.0 collective-permute-done.3
  35.8 0.0 collective-permute-done.4
  35.8 0.0 collective-permute-done.5
  35.8 0.0 collective-permute-done.6
  35.8 0.0 collective-permute-done.7
  35.9 0.8 %add_bitcast_fusion = f32[1,16,4096]{2,1,0:T(8,128)} fusion(bf16[16,4096]{1,0:T(8,128)(2,1)S(1)} %collective-permute-done.7, bf16[16,4096]{1,0:T(8,128)(2,1)S(1)} %collective-permute-done.6, bf16[16,4096]{1,0:T(8,128)(2,1)S(1)} %collective-permute-done.5, bf16[16,4096]{1,0:T(8,128)(2,1)S(1)} %collective-permute-done.4, ...), kind=kLoop, calls=%fused_computation | loop fusion | flops 786432 | bytes 1310720 | tf_op jit(solution)/shard_map/broadcast_in_dim | solution.py:299
  (1 shorter events, 0.0 us)
Async XLA Ops:
  1.8 21.0 %collective-permute-start.1 = (bf16[64,4224]{1,0:T(8,128)(2,1)S(1)}, bf16[64,4224]{1,0:T(8,128)(2,1)S(1)}, u32[]{:S(2)}, u32[]{:S(2)}) collective-permute-start(bf16[64,4224]{1,0:T(8,128)(2,1)S(1)} %pack.1.refs_1_), channel_id=1, source_target_pairs={{4,0},{5,1},{6,2},{7,3},{8,4},{9,5},{10,6},{11,7},{12,8},{13,9},{1... | collective-permute-start | bytes 1622024 | tf_op jit(solution)/shard_map/ppermute | solution.py:247
  6.6 27.1 %collective-permute-start = (bf16[64,4224]{1,0:T(8,128)(2,1)S(1)}, bf16[64,4224]{1,0:T(8,128)(2,1)S(1)}, u32[]{:S(2)}, u32[]{:S(2)}) collective-permute-start(bf16[64,4224]{1,0:T(8,128)(2,1)S(1)} %pack.1.refs_1_), channel_id=1, source_target_pairs={{0,766},{1,767},{2,764},{3,765},{764,760},{765,761},{766,762},{767... | collective-permute-start | bytes 1622024 | tf_op jit(solution)/shard_map/ppermute | solution.py:247
  24.5 10.6 %collective-permute-start.2 = (bf16[16,4096]{1,0:T(8,128)(2,1)S(1)}, bf16[16,4096]{1,0:T(8,128)(2,1)S(1)}, u32[]{:S(2)}, u32[]{:S(2)}) collective-permute-start(bf16[16,4096]{1,0:T(8,128)(2,1)S(1)} %get-tuple-element.35), channel_id=1, source_target_pairs={{0,2},{1,3},{2,0},{3,1},{4,6},{5,7},{6,4},{7,5},{8,10},{9,11},{10,... | collective-permute-start | bytes 393224 | tf_op jit(solution)/shard_map/ppermute | solution.py:247
  26.5 9.3 %collective-permute-start.3 = (bf16[16,4096]{1,0:T(8,128)(2,1)S(1)}, bf16[16,4096]{1,0:T(8,128)(2,1)S(1)}, u32[]{:S(2)}, u32[]{:S(2)}) collective-permute-start(bf16[16,4096]{1,0:T(8,128)(2,1)S(1)} %get-tuple-element.36), channel_id=1, source_target_pairs={{0,3},{1,2},{2,1},{3,0},{4,7},{5,6},{6,5},{7,4},{8,11},{9,10},{10,... | collective-permute-start | bytes 393224 | tf_op jit(solution)/shard_map/ppermute | solution.py:247
  31.0 4.8 %collective-permute-start.4 = (bf16[16,4096]{1,0:T(8,128)(2,1)S(1)}, bf16[16,4096]{1,0:T(8,128)(2,1)S(1)}, u32[]{:S(2)}, u32[]{:S(2)}) collective-permute-start(bf16[16,4096]{1,0:T(8,128)(2,1)S(1)} %get-tuple-element.37), channel_id=1, source_target_pairs={{0,1},{1,0},{2,3},{3,2},{4,5},{5,4},{6,7},{7,6},{8,9},{9,8},{10,11... | collective-permute-start | bytes 393224 | tf_op jit(solution)/shard_map/ppermute | solution.py:247
  33.8 2.1 %collective-permute-start.5 = (bf16[16,4096]{1,0:T(8,128)(2,1)S(1)}, bf16[16,4096]{1,0:T(8,128)(2,1)S(1)}, u32[]{:S(2)}, u32[]{:S(2)}) collective-permute-start(bf16[16,4096]{1,0:T(8,128)(2,1)S(1)} %get-tuple-element.38), channel_id=1, source_target_pairs={{760,762},{761,763},{762,760},{763,761},{764,766},{765,767},{766,7... | collective-permute-start | bytes 393224 | tf_op jit(solution)/shard_map/ppermute | solution.py:247
  34.4 1.4 %collective-permute-start.6 = (bf16[16,4096]{1,0:T(8,128)(2,1)S(1)}, bf16[16,4096]{1,0:T(8,128)(2,1)S(1)}, u32[]{:S(2)}, u32[]{:S(2)}) collective-permute-start(bf16[16,4096]{1,0:T(8,128)(2,1)S(1)} %get-tuple-element.39), channel_id=1, source_target_pairs={{760,763},{761,762},{762,761},{763,760},{764,767},{765,766},{766,7... | collective-permute-start | bytes 393224 | tf_op jit(solution)/shard_map/ppermute | solution.py:247
  35.1 0.7 %collective-permute-start.7 = (bf16[16,4096]{1,0:T(8,128)(2,1)S(1)}, bf16[16,4096]{1,0:T(8,128)(2,1)S(1)}, u32[]{:S(2)}, u32[]{:S(2)}) collective-permute-start(bf16[16,4096]{1,0:T(8,128)(2,1)S(1)} %get-tuple-element.40), channel_id=1, source_target_pairs={{760,761},{761,760},{762,763},{763,762},{764,765},{765,764},{766,7... | collective-permute-start | bytes 393224 | tf_op jit(solution)/shard_map/ppermute | solution.py:247

commit v6 on v5

--- a/solution.py
+++ b/solution.py
@@ -8,6 +8,7 @@
 from jax.experimental.pallas import tpu as pltpu
 from jax.sharding import PartitionSpec as P
 
+
 SCREEN_SQUARE = 16.0
 N = 64
 HALF = 32
@@ -15,6 +16,7 @@
 WIDE = 256
 BLOCKS = N * N // WIDE
 STRIDE = 65
+TURNED_ROWS = HALF * STRIDE + N + 8
 CHUNK = 256
 MEMBERS = 4
 SLAB = N // MEMBERS
@@ -187,45 +189,65 @@
         own_body(count, *refs)
 
 
-def cross_body(count, target, packed, field, kernel, table, mine, sent, scratch):
+def cross_body(count, target, packed, field, kernel, table, scratch, emit_total):
     def emit(block, value):
-        total = field[:, columns_of(block)] + value
-        mine[:, columns_of(block)] = total[:SLAB]
-        for k in range(1, MEMBERS):
-            sent[k - 1][:, columns_of(block)] = total[k * SLAB : (k + 1) * SLAB].astype(jnp.bfloat16)
+        emit_total(columns_of(block), field[:, columns_of(block)] + value)
 
     pair_field(
         lax.axis_index("group"), target, packed, minus_occupation(count, packed), lambda: kernel, table, *scratch, emit
     )
 
 
+def slab(total, k):
+    return total[k * SLAB : (k + 1) * SLAB]
+
+
 def cross_kernel(count, target, packed, field, kernel, table, mine, *rest):
+    sent, scratch = rest[: MEMBERS - 1], rest[MEMBERS - 1 :]
+
+    def emit_total(columns, total):
+        mine[:, columns] = slab(total, 0)
+        for k in range(1, MEMBERS):
+            sent[k - 1][:, columns] = slab(total, k).astype(jnp.bfloat16)
+
     @pl.when(jnp.logical_not(on_late_band()))
     def _():
-        cross_body(count, target, packed, field, kernel, table, mine, rest[: MEMBERS - 1], rest[MEMBERS - 1 :])
-
-
-def cross_late_kernel(count, target, packed, field, kernel, table, held, mine, *rest):
+        cross_body(count, target, packed, field, kernel, table, scratch, emit_total)
+
+
+def cross_late_kernel(count, target, packed, field, kernel, table, held, mine, kept, sent, *scratch):
+    def emit_total(columns, total):
+        mine[:, columns] = slab(total, 0)
+        kept[:, columns] = slab(total, 2)
+        sent[:SLAB, columns] = slab(total, 1).astype(jnp.bfloat16)
+        sent[SLAB:, columns] = slab(total, 3).astype(jnp.bfloat16)
+
     @pl.when(on_late_band())
     def _():
-        cross_body(count, target, packed, field, kernel, table, mine, rest[: MEMBERS - 1], rest[MEMBERS - 1 :])
+        cross_body(count, target, packed, field, kernel, table, scratch, emit_total)
 
     @pl.when(jnp.logical_not(on_late_band()))
     def _():
         mine[...] = held[...]
+
+
+def chip_sum_kernel(kept, got, sent):
+    @pl.when(on_late_band())
+    def _():
+        sent[...] = (kept[...] + got[SLAB:, :].astype(jnp.float32)).astype(jnp.bfloat16)
 
 
 def shape(rows, columns, dtype):
     return jax.ShapeDtypeStruct((rows, columns), dtype)
 
 
-PAIR_SCRATCH = [pltpu.VMEM((HALF * STRIDE, LANES), jnp.float32), pltpu.VMEM((BLOCKS * N, WIDE), jnp.bfloat16)]
+PAIR_SCRATCH = [pltpu.VMEM((TURNED_ROWS, LANES), jnp.float32), pltpu.VMEM((BLOCKS * N, WIDE), jnp.bfloat16)]
 OWN_SCRATCH = [pltpu.VMEM((N, N * N), jnp.int32)] + PAIR_SCRATCH + [pltpu.SemaphoreType.DMA((3,))]
 VMEM = pl.BlockSpec(memory_space=pltpu.VMEM)
 HBM = pl.BlockSpec(memory_space=pltpu.HBM)
 
 
-def call(kernel, outs, in_specs, scratch, name, aliases=None, flops=6 * 2 * N**4):
+def call(kernel, outs, in_specs, scratch, aliases=None, flops=6 * 2 * N**4):
     return pl.pallas_call(
         kernel,
         out_shape=outs,
@@ -235,7 +257,6 @@
         input_output_aliases=aliases or {},
         compiler_params=pltpu.CompilerParams(vmem_limit_bytes=40 * 1024 * 1024),
         cost_estimate=pl.CostEstimate(flops=flops, bytes_accessed=4 * 1024 * 1024, transcendentals=0),
-        name=name,
     )
 
 
@@ -252,10 +273,8 @@
     return [((b, g), ((b - 1) % count, g ^ 2 if b % ROW == 0 else g)) for b in bands for g in range(MEMBERS)]
 
 
-def exchanged(sent, bands):
-    return [
-        sent_along(sent[bits - 1], [((b, g), (b, g ^ bits)) for b in bands for g in range(MEMBERS)]) for bits in (2, 3, 1)
-    ]
+def swapped(value, bits, bands):
+    return sent_along(value, [((b, g), (b, g ^ bits)) for b in bands for g in range(MEMBERS)])
 
 
 def shards(trial, orbitals, labels, kernel_mask):
@@ -267,7 +286,6 @@
         [shape(N, PACKED, jnp.bfloat16)],
         [pl.BlockSpec(memory_space=pltpu.SMEM), HBM],
         [pltpu.SemaphoreType.DMA((PACK_COPIES,))],
-        "pack",
         flops=0,
     )(labels, in_hbm(orbitals[0]))[0]
     following = sent_along(packed, next_sources(range(1, bands - 1)))
@@ -279,22 +297,28 @@
     ]
     sources = [HBM, VMEM, HBM, HBM]
     field, kernel, kept_target, kept_table = call(
-        functools.partial(own_kernel, count), planes, sources, OWN_SCRATCH, "own"
+        functools.partial(own_kernel, count), planes, sources, OWN_SCRATCH
     )(target, packed, mask, table)
     packed, field = lax.optimization_barrier((packed, field))
     wrapped = sent_along(packed, next_sources((0, bands - 1)))
     late_field, late_kernel, late_target, late_table = call(
-        functools.partial(own_late_kernel, count), planes, sources, OWN_SCRATCH, "own_late"
+        functools.partial(own_late_kernel, count), planes, sources, OWN_SCRATCH
     )(target, packed, mask, table)
     slabs = [shape(SLAB, N * N, jnp.float32)] + [shape(SLAB, N * N, jnp.bfloat16)] * (MEMBERS - 1)
-    mine, *sent = call(functools.partial(cross_kernel, count), slabs, [VMEM] * 5, PAIR_SCRATCH, "cross")(
+    mine, *sent = call(functools.partial(cross_kernel, count), slabs, [VMEM] * 5, PAIR_SCRATCH)(
         kept_target, following, field, kernel, kept_table
     )
-    received = exchanged(sent, range(bands - LATE))
-    mine, *sent = call(
-        functools.partial(cross_late_kernel, count), slabs, [VMEM] * 6, PAIR_SCRATCH, "cross_late", aliases={5: 0}
+    received = []
+    for bits in (2, 3, 1):
+        received.append(swapped(sent[bits - 1], bits, range(bands - LATE)))
+    late_bands = range(bands - LATE, bands)
+    late_slabs = [shape(SLAB, N * N, jnp.float32)] * 2 + [shape(2 * SLAB, N * N, jnp.bfloat16)]
+    mine, kept, sent = call(
+        functools.partial(cross_late_kernel, count), late_slabs, [VMEM] * 6, PAIR_SCRATCH, aliases={5: 0}
     )(late_target, wrapped, late_field, late_kernel, late_table, mine)
-    for piece in received + exchanged(sent, range(bands - LATE, bands)):
+    near = swapped(sent, 1, late_bands)
+    far = call(chip_sum_kernel, [shape(SLAB, N * N, jnp.bfloat16)], [VMEM] * 2, [], flops=0)(kept, near)[0]
+    for piece in received + [near[:SLAB], swapped(far, 2, late_bands)]:
         mine = mine + piece.astype(jnp.float32)
     return mine[None]
 

time: 37 us -> 46.2 us (1.25)
  waiting for transfers between devices: 0.83 us -> 10.2 us
    ppermute x8 -> x7, waiting for transfers between devices: 0.83 us -> 10.2 us  [sent_along(): lax.ppermute(value, ('band', 'group'), [(s[0] * MEMBERS + s[1], t[0] * ME...]
    ppermute x8 -> x7, starting transfers between devices: 27.8 us -> 27.7 us  [sent_along(): lax.ppermute(value, ('band', 'group'), [(s[0] * MEMBERS + s[1], t[0] * ME...]
    pallas_call x2 -> x3, Pallas kernels: 3.57 us -> 3.6 us  [the longest x1 3.55 us: shards(): call(functools.partial(own_kernel, count), planes, sources, OWN_SCRATCH)]
  transfers between devices with their start and end apart: 8 -> 7, of which waited for: 1 -> 2; matrix products, arithmetic and copies ran while one was open for 0% -> 0% of each run, Pallas kernels for 14% -> 12%
where the time goes in v6:
time: 46.2 us; the launch traced here: 45.9 us
  starting transfers between devices  27.7 us (60%)
  waiting for transfers between devices  10.2 us (22%)
  Pallas kernels  6.47 us (14%)
  other arithmetic  0.79 us (2%)
  between operations  0.78 us (2%)
    ppermute x7, starting transfers between devices, sent_along(): lax.ppermute(value, ('band', 'group'), [(s[0] * MEMBERS + s[1], t[0] * ME...  27.7 us
    ppermute x7, waiting for transfers between devices, sent_along(): lax.ppermute(value, ('band', 'group'), [(s[0] * MEMBERS + s[1], t[0] * ME...  10.2 us
    pallas_call x1, Pallas kernels, shards(): call(functools.partial(own_kernel, count), planes, sources, OWN_SCRATCH)  3.55 us
    pallas_call x1, Pallas kernels, shards(): call(functools.partial(cross_kernel, count), slabs, [VMEM] * 5, PAIR_SCRA...  1.69 us
    pallas_call x1, Pallas kernels, shards(): call(pack_kernel, [shape(N, PACKED, jnp.bfloat16)], [pl.BlockSpec(memory_...  1.13 us
  transfers between devices with their start and end apart: 7, of which 2 were waited for; matrix products, arithmetic and copies ran while one was open for 0% of the time, Pallas kernels for 12%

profile of v6, /device:TPU:1, one launch (start us, length us, event | category | flops | bytes accessed | tf_op | source)
XLA Modules:
  0.0 45.9 jit_solution(1738664489758080850)
XLA Ops:
  0.7 1.1 %shard_map.55.refs_1_ = bf16[64,4224]{1,0:T(8,128)(2,1)S(1)} custom-call(s32[1]{0:T(128)S(6)} %copy.8.label, bf16[64,4096]{1,0:T(8,128)(2,1)} %bitcast.6), custom_call_target="tpu_custom_call" | custom-call | bytes 4194304 | tf_op jit(solution)/shard_map/pallas_call | solution.py:284
  1.8 1.3 %collective-permute-start.1 = (bf16[64,4224]{1,0:T(8,128)(2,1)S(1)}, bf16[64,4224]{1,0:T(8,128)(2,1)S(1)}, u32[]{:S(2)}, u32[]{:S(2)}) collective-permute-start(bf16[64,4224]{1,0:T(8,128)(2,1)S(1)} %shard_map.55.refs_1_), channel_id=1, source_target_pairs={{4,0},{5,1},{6,2},{7,3},{8,4},{9,5},{10,6},{11,7},{12,8},{13,9},{1... | collective-permute-start | bytes 1622024 | tf_op jit(solution)/shard_map/ppermute | solution.py:268
  3.1 3.5 %shard_map.56 = (f32[64,4096]{1,0:T(8,128)S(1)}, f32[1024,256]{1,0:T(8,128)S(1)}, bf16[64,4096]{1,0:T(8,128)(2,1)S(1)}, bf16[512,256]{1,0:T(8,128)(2,1)S(1)}) custom-call(bf16[64,4096]{1,0:T(8,128)(2,1)} %bitcast.4, bf16[64,4224]{1,0:T(8,128)(2,1)S(1)} %shard_map.55.refs_1_, s32[64,4096]{1,0:T(8,128)} %refs_2_.3, bf16[512,256]{1,0:T(8,128)(2,1)} %constant.2.clone.refs_3_), custom_call_target="tpu_custom_call" | custom-call | flops 201326592 | bytes 4194304 | tf_op jit(solution)/shard_map/pallas_call | solution.py:299
  6.6 16.2 %collective-permute-start = (bf16[64,4224]{1,0:T(8,128)(2,1)S(1)}, bf16[64,4224]{1,0:T(8,128)(2,1)S(1)}, u32[]{:S(2)}, u32[]{:S(2)}) collective-permute-start(bf16[64,4224]{1,0:T(8,128)(2,1)S(1)} %shard_map.55.refs_1_), channel_id=1, source_target_pairs={{0,766},{1,767},{2,764},{3,765},{764,760},{765,761},{766,762},{767... | collective-permute-start | bytes 1622024 | tf_op jit(solution)/shard_map/ppermute | solution.py:268
  22.8 0.1 shard_map.57
  22.9 0.0 collective-permute-done.1.packed
  22.9 1.7 %shard_map.58 = (f32[16,4096]{1,0:T(8,128)S(1)}, bf16[16,4096]{1,0:T(8,128)(2,1)S(1)}, bf16[16,4096]{1,0:T(8,128)(2,1)S(1)}, bf16[16,4096]{1,0:T(8,128)(2,1)S(1)}) custom-call(bf16[64,4096]{1,0:T(8,128)(2,1)S(1)} %get-tuple-element.28.target, bf16[64,4224]{1,0:T(8,128)(2,1)S(1)} %collective-permute-done.1.packed, f32[64,4096]{1,0:T(8,128)S(1)} %get-tuple-element.29.field, ...), custom_call_target="tpu_custom_call" | custom-call | flops 201326592 | bytes 4194304 | tf_op jit(solution)/shard_map/pallas_call | solution.py:308
  24.6 9.1 %collective-permute-done.packed = bf16[64,4224]{1,0:T(8,128)(2,1)S(1)} collective-permute-done((bf16[64,4224]{1,0:T(8,128)(2,1)S(1)}, bf16[64,4224]{1,0:T(8,128)(2,1)S(1)}, u32[]{:S(2)}, u32[]{:S(2)}) %collective-permute-start) | collective-permute-done | bytes 540704 | tf_op jit(solution)/shard_map/ppermute | solution.py:268
  33.8 0.7 %collective-permute-start.5 = (bf16[32,4096]{1,0:T(8,128)(2,1)S(1)}, bf16[32,4096]{1,0:T(8,128)(2,1)S(1)}, u32[]{:S(2)}, u32[]{:S(2)}) collective-permute-start(bf16[32,4096]{1,0:T(8,128)(2,1)S(1)} %get-tuple-element.37), channel_id=1, source_target_pairs={{760,761},{761,760},{762,763},{763,762},{764,765},{765,764},{766,7... | collective-permute-start | bytes 786440 | tf_op jit(solution)/shard_map/ppermute | solution.py:268
  34.4 1.9 %collective-permute-start.2 = (bf16[16,4096]{1,0:T(8,128)(2,1)S(1)}, bf16[16,4096]{1,0:T(8,128)(2,1)S(1)}, u32[]{:S(2)}, u32[]{:S(2)}) collective-permute-start(bf16[16,4096]{1,0:T(8,128)(2,1)S(1)} %get-tuple-element.34), channel_id=1, source_target_pairs={{0,2},{1,3},{2,0},{3,1},{4,6},{5,7},{6,4},{7,5},{8,10},{9,11},{10,... | collective-permute-start | bytes 393224 | tf_op jit(solution)/shard_map/ppermute | solution.py:268
  36.4 5.1 %collective-permute-start.3 = (bf16[16,4096]{1,0:T(8,128)(2,1)S(1)}, bf16[16,4096]{1,0:T(8,128)(2,1)S(1)}, u32[]{:S(2)}, u32[]{:S(2)}) collective-permute-start(bf16[16,4096]{1,0:T(8,128)(2,1)S(1)} %get-tuple-element.35), channel_id=1, source_target_pairs={{0,3},{1,2},{2,1},{3,0},{4,7},{5,6},{6,5},{7,4},{8,11},{9,10},{10,... | collective-permute-start | bytes 393224 | tf_op jit(solution)/shard_map/ppermute | solution.py:268
  41.4 1.9 %collective-permute-start.4 = (bf16[16,4096]{1,0:T(8,128)(2,1)S(1)}, bf16[16,4096]{1,0:T(8,128)(2,1)S(1)}, u32[]{:S(2)}, u32[]{:S(2)}) collective-permute-start(bf16[16,4096]{1,0:T(8,128)(2,1)S(1)} %get-tuple-element.36), channel_id=1, source_target_pairs={{0,1},{1,0},{2,3},{3,2},{4,5},{5,4},{6,7},{7,6},{8,9},{9,8},{10,11... | collective-permute-start | bytes 393224 | tf_op jit(solution)/shard_map/ppermute | solution.py:268
  43.4 0.0 collective-permute-done.5.got
  43.4 0.7 %collective-permute-start.6 = (bf16[16,4096]{1,0:T(8,128)(2,1)S(1)}, bf16[16,4096]{1,0:T(8,128)(2,1)S(1)}, u32[]{:S(2)}, u32[]{:S(2)}) collective-permute-start(bf16[16,4096]{1,0:T(8,128)(2,1)S(1)} %shard_map.60), channel_id=1, source_target_pairs={{760,762},{761,763},{762,760},{763,761},{764,766},{765,767},{766,7... | collective-permute-start | bytes 393224 | tf_op jit(solution)/shard_map/ppermute | solution.py:268
  44.1 0.0 collective-permute-done.2
  44.1 1.0 %collective-permute-done.3 = bf16[16,4096]{1,0:T(8,128)(2,1)S(1)} collective-permute-done((bf16[16,4096]{1,0:T(8,128)(2,1)S(1)}, bf16[16,4096]{1,0:T(8,128)(2,1)S(1)}, u32[]{:S(2)}, u32[]{:S(2)}) %collective-permute-start.3) | collective-permute-done | bytes 131104 | tf_op jit(solution)/shard_map/ppermute | solution.py:268
  45.1 0.0 collective-permute-done.4
  45.1 0.0 collective-permute-done.6
  45.1 0.8 %add_bitcast_fusion = f32[1,16,4096]{2,1,0:T(8,128)} fusion(bf16[16,4096]{1,0:T(8,128)(2,1)S(1)} %collective-permute-done.6, bf16[16,4096]{1,0:T(8,128)(2,1)S(1)} %collective-permute-done.4, bf16[16,4096]{1,0:T(8,128)(2,1)S(1)} %collective-permute-done.3, f32[16,4096]{1,0:T(8,128)S(1)} %get-tuple-element.33, bf16[16,4096]{1,0:T(8,128)(2,1)S(1)} %collective-permute-done.2, ...), kind=kLoop, calls=%fused_computation | loop fusion | flops 655360 | bytes 1179648 | tf_op jit(solution)/shard_map/broadcast_in_dim | solution.py:323
  (2 shorter events, 0.1 us)
Async XLA Ops:
  1.8 21.1 %collective-permute-start.1 = (bf16[64,4224]{1,0:T(8,128)(2,1)S(1)}, bf16[64,4224]{1,0:T(8,128)(2,1)S(1)}, u32[]{:S(2)}, u32[]{:S(2)}) collective-permute-start(bf16[64,4224]{1,0:T(8,128)(2,1)S(1)} %shard_map.55.refs_1_), channel_id=1, source_target_pairs={{4,0},{5,1},{6,2},{7,3},{8,4},{9,5},{10,6},{11,7},{12,8},{13,9},{1... | collective-permute-start | bytes 1622024 | tf_op jit(solution)/shard_map/ppermute | solution.py:268
  6.6 27.1 %collective-permute-start = (bf16[64,4224]{1,0:T(8,128)(2,1)S(1)}, bf16[64,4224]{1,0:T(8,128)(2,1)S(1)}, u32[]{:S(2)}, u32[]{:S(2)}) collective-permute-start(bf16[64,4224]{1,0:T(8,128)(2,1)S(1)} %shard_map.55.refs_1_), channel_id=1, source_target_pairs={{0,766},{1,767},{2,764},{3,765},{764,760},{765,761},{766,762},{767... | collective-permute-start | bytes 1622024 | tf_op jit(solution)/shard_map/ppermute | solution.py:268
  33.8 9.6 %collective-permute-start.5 = (bf16[32,4096]{1,0:T(8,128)(2,1)S(1)}, bf16[32,4096]{1,0:T(8,128)(2,1)S(1)}, u32[]{:S(2)}, u32[]{:S(2)}) collective-permute-start(bf16[32,4096]{1,0:T(8,128)(2,1)S(1)} %get-tuple-element.37), channel_id=1, source_target_pairs={{760,761},{761,760},{762,763},{763,762},{764,765},{765,764},{766,7... | collective-permute-start | bytes 786440 | tf_op jit(solution)/shard_map/ppermute | solution.py:268
  34.4 9.6 %collective-permute-start.2 = (bf16[16,4096]{1,0:T(8,128)(2,1)S(1)}, bf16[16,4096]{1,0:T(8,128)(2,1)S(1)}, u32[]{:S(2)}, u32[]{:S(2)}) collective-permute-start(bf16[16,4096]{1,0:T(8,128)(2,1)S(1)} %get-tuple-element.34), channel_id=1, source_target_pairs={{0,2},{1,3},{2,0},{3,1},{4,6},{5,7},{6,4},{7,5},{8,10},{9,11},{10,... | collective-permute-start | bytes 393224 | tf_op jit(solution)/shard_map/ppermute | solution.py:268
  36.4 8.7 %collective-permute-start.3 = (bf16[16,4096]{1,0:T(8,128)(2,1)S(1)}, bf16[16,4096]{1,0:T(8,128)(2,1)S(1)}, u32[]{:S(2)}, u32[]{:S(2)}) collective-permute-start(bf16[16,4096]{1,0:T(8,128)(2,1)S(1)} %get-tuple-element.35), channel_id=1, source_target_pairs={{0,3},{1,2},{2,1},{3,0},{4,7},{5,6},{6,5},{7,4},{8,11},{9,10},{10,... | collective-permute-start | bytes 393224 | tf_op jit(solution)/shard_map/ppermute | solution.py:268
  41.4 3.7 %collective-permute-start.4 = (bf16[16,4096]{1,0:T(8,128)(2,1)S(1)}, bf16[16,4096]{1,0:T(8,128)(2,1)S(1)}, u32[]{:S(2)}, u32[]{:S(2)}) collective-permute-start(bf16[16,4096]{1,0:T(8,128)(2,1)S(1)} %get-tuple-element.36), channel_id=1, source_target_pairs={{0,1},{1,0},{2,3},{3,2},{4,5},{5,4},{6,7},{7,6},{8,9},{9,8},{10,11... | collective-permute-start | bytes 393224 | tf_op jit(solution)/shard_map/ppermute | solution.py:268
  43.4 1.7 %collective-permute-start.6 = (bf16[16,4096]{1,0:T(8,128)(2,1)S(1)}, bf16[16,4096]{1,0:T(8,128)(2,1)S(1)}, u32[]{:S(2)}, u32[]{:S(2)}) collective-permute-start(bf16[16,4096]{1,0:T(8,128)(2,1)S(1)} %shard_map.60), channel_id=1, source_target_pairs={{760,762},{761,763},{762,760},{763,761},{764,766},{765,767},{766,7... | collective-permute-start | bytes 393224 | tf_op jit(solution)/shard_map/ppermute | solution.py:268

commit v7 on v5

--- a/solution.py
+++ b/solution.py
@@ -8,6 +8,7 @@
 from jax.experimental.pallas import tpu as pltpu
 from jax.sharding import PartitionSpec as P
 
+
 SCREEN_SQUARE = 16.0
 N = 64
 HALF = 32
@@ -15,6 +16,7 @@
 WIDE = 256
 BLOCKS = N * N // WIDE
 STRIDE = 65
+TURNED_ROWS = HALF * STRIDE + N + 8
 CHUNK = 256
 MEMBERS = 4
 SLAB = N // MEMBERS
@@ -109,26 +111,32 @@
         emit(block, potential * scale * by_owner(me, source, columns_of(block)).astype(jnp.float32))
 
 
+def on_last_band():
+    return lax.axis_index("band") == lax.axis_size("band") - 1
+
+
 def on_late_band():
     return lax.axis_index("band") >= lax.axis_size("band") - LATE
 
 
-def pack_kernel(label, source, packed, sems):
-    step = N * N // PACK_COPIES
-    copies = [
-        pltpu.make_async_copy(
-            source.at[:, i * step : (i + 1) * step], packed.at[:, i * step : (i + 1) * step], sems.at[i]
-        )
-        for i in range(PACK_COPIES)
-    ]
-    for copy in copies:
-        copy.start()
-    for half, part in enumerate((label[0] // 8, label[0] % 8)):
-        packed[half * HALF : (half + 1) * HALF, N * N :] = (
-            jnp.full((HALF, LANES), part, jnp.int32).astype(jnp.float32).astype(jnp.bfloat16)
-        )
-    for copy in copies:
-        copy.wait()
+def pack_kernel(late, label, source, packed, sems):
+    @pl.when(on_late_band() if late else jnp.logical_not(on_last_band()))
+    def _():
+        step = N * N // PACK_COPIES
+        copies = [
+            pltpu.make_async_copy(
+                source.at[:, i * step : (i + 1) * step], packed.at[:, i * step : (i + 1) * step], sems.at[i]
+            )
+            for i in range(PACK_COPIES)
+        ]
+        for copy in copies:
+            copy.start()
+        for half, part in enumerate((label[0] // 8, label[0] % 8)):
+            packed[half * HALF : (half + 1) * HALF, N * N :] = (
+                jnp.full((HALF, LANES), part, jnp.int32).astype(jnp.float32).astype(jnp.bfloat16)
+            )
+        for copy in copies:
+            copy.wait()
 
 
 def minus_occupation(count, packed):
@@ -205,10 +213,15 @@
         cross_body(count, target, packed, field, kernel, table, mine, rest[: MEMBERS - 1], rest[MEMBERS - 1 :])
 
 
-def cross_late_kernel(count, target, packed, field, kernel, table, held, mine, *rest):
-    @pl.when(on_late_band())
-    def _():
-        cross_body(count, target, packed, field, kernel, table, mine, rest[: MEMBERS - 1], rest[MEMBERS - 1 :])
+def cross_late_kernel(count, target, from_first, from_last, field, kernel, table, held, mine, *rest):
+    for packed, here in (
+        (from_first, on_last_band()),
+        (from_last, jnp.logical_and(on_late_band(), jnp.logical_not(on_last_band()))),
+    ):
+
+        @pl.when(here)
+        def _():
+            cross_body(count, target, packed, field, kernel, table, mine, rest[: MEMBERS - 1], rest[MEMBERS - 1 :])
 
     @pl.when(jnp.logical_not(on_late_band()))
     def _():
@@ -219,13 +232,13 @@
     return jax.ShapeDtypeStruct((rows, columns), dtype)
 
 
-PAIR_SCRATCH = [pltpu.VMEM((HALF * STRIDE, LANES), jnp.float32), pltpu.VMEM((BLOCKS * N, WIDE), jnp.bfloat16)]
+PAIR_SCRATCH = [pltpu.VMEM((TURNED_ROWS, LANES), jnp.float32), pltpu.VMEM((BLOCKS * N, WIDE), jnp.bfloat16)]
 OWN_SCRATCH = [pltpu.VMEM((N, N * N), jnp.int32)] + PAIR_SCRATCH + [pltpu.SemaphoreType.DMA((3,))]
 VMEM = pl.BlockSpec(memory_space=pltpu.VMEM)
 HBM = pl.BlockSpec(memory_space=pltpu.HBM)
 
 
-def call(kernel, outs, in_specs, scratch, name, aliases=None, flops=6 * 2 * N**4):
+def call(kernel, outs, in_specs, scratch, aliases=None, flops=6 * 2 * N**4):
     return pl.pallas_call(
         kernel,
         out_shape=outs,
@@ -235,7 +248,6 @@
         input_output_aliases=aliases or {},
         compiler_params=pltpu.CompilerParams(vmem_limit_bytes=40 * 1024 * 1024),
         cost_estimate=pl.CostEstimate(flops=flops, bytes_accessed=4 * 1024 * 1024, transcendentals=0),
-        name=name,
     )
 
 
@@ -253,23 +265,29 @@
 
 
 def exchanged(sent, bands):
-    return [
-        sent_along(sent[bits - 1], [((b, g), (b, g ^ bits)) for b in bands for g in range(MEMBERS)]) for bits in (2, 3, 1)
-    ]
+    received = []
+    for bits in (2, 3, 1):
+        pairs = [((b, g), (b, g ^ bits)) for b in bands for g in range(MEMBERS)]
+        received.append(sent_along(sent[bits - 1], pairs))
+    return received
 
 
 def shards(trial, orbitals, labels, kernel_mask):
     bands = lax.axis_size("band")
     count = bands * MEMBERS
     target, table, mask = in_hbm(trial[0]), in_hbm(tables()), in_hbm(kernel_mask)
-    packed = call(
-        pack_kernel,
-        [shape(N, PACKED, jnp.bfloat16)],
-        [pl.BlockSpec(memory_space=pltpu.SMEM), HBM],
-        [pltpu.SemaphoreType.DMA((PACK_COPIES,))],
-        "pack",
-        flops=0,
-    )(labels, in_hbm(orbitals[0]))[0]
+    source = in_hbm(orbitals[0])
+
+    def packing(late):
+        return call(
+            functools.partial(pack_kernel, late),
+            [shape(N, PACKED, jnp.bfloat16)],
+            [pl.BlockSpec(memory_space=pltpu.SMEM), HBM],
+            [pltpu.SemaphoreType.DMA((PACK_COPIES,))],
+            flops=0,
+        )
+
+    packed = packing(False)(labels, source)[0]
     following = sent_along(packed, next_sources(range(1, bands - 1)))
     planes = [
         shape(N, N * N, jnp.float32),
@@ -279,21 +297,23 @@
     ]
     sources = [HBM, VMEM, HBM, HBM]
     field, kernel, kept_target, kept_table = call(
-        functools.partial(own_kernel, count), planes, sources, OWN_SCRATCH, "own"
+        functools.partial(own_kernel, count), planes, sources, OWN_SCRATCH
     )(target, packed, mask, table)
     packed, field = lax.optimization_barrier((packed, field))
-    wrapped = sent_along(packed, next_sources((0, bands - 1)))
+    from_first = sent_along(packed, next_sources((0,)))
+    late_packed = packing(True)(labels, source)[0]
+    from_last = sent_along(late_packed, next_sources((bands - 1,)))
     late_field, late_kernel, late_target, late_table = call(
-        functools.partial(own_late_kernel, count), planes, sources, OWN_SCRATCH, "own_late"
-    )(target, packed, mask, table)
+        functools.partial(own_late_kernel, count), planes, sources, OWN_SCRATCH
+    )(target, late_packed, mask, table)
     slabs = [shape(SLAB, N * N, jnp.float32)] + [shape(SLAB, N * N, jnp.bfloat16)] * (MEMBERS - 1)
-    mine, *sent = call(functools.partial(cross_kernel, count), slabs, [VMEM] * 5, PAIR_SCRATCH, "cross")(
+    mine, *sent = call(functools.partial(cross_kernel, count), slabs, [VMEM] * 5, PAIR_SCRATCH)(
         kept_target, following, field, kernel, kept_table
     )
     received = exchanged(sent, range(bands - LATE))
     mine, *sent = call(
-        functools.partial(cross_late_kernel, count), slabs, [VMEM] * 6, PAIR_SCRATCH, "cross_late", aliases={5: 0}
-    )(late_target, wrapped, late_field, late_kernel, late_table, mine)
+        functools.partial(cross_late_kernel, count), slabs, [VMEM] * 7, PAIR_SCRATCH, aliases={6: 0}
+    )(late_target, from_first, from_last, late_field, late_kernel, late_table, mine)
     for piece in received + exchanged(sent, range(bands - LATE, bands)):
         mine = mine + piece.astype(jnp.float32)
     return mine[None]

time: 37 us -> 46.5 us (1.26)
  waiting for transfers between devices: 0.83 us -> 10.1 us
    ppermute x8 -> x9, waiting for transfers between devices: 0.83 us -> 10.1 us  [sent_along(): lax.ppermute(value, ('band', 'group'), [(s[0] * MEMBERS + s[1], t[0] * ME...]
    ppermute x8 -> x9, starting transfers between devices: 27.8 us -> 28 us  [sent_along(): lax.ppermute(value, ('band', 'group'), [(s[0] * MEMBERS + s[1], t[0] * ME...]
    pallas_call x3 -> x4, Pallas kernels: 4.7 us -> 4.78 us  [the longest x1 3.55 us: shards(): call(functools.partial(own_kernel, count), planes, sources, OWN_SCRATCH)]
  transfers between devices with their start and end apart: 8 -> 9, of which waited for: 1 -> 2; matrix products, arithmetic and copies ran while one was open for 0% -> 0% of each run, Pallas kernels for 14% -> 12%
where the time goes in v7:
time: 46.5 us; the launch traced here: 46.2 us
  starting transfers between devices  28 us (60%)
  waiting for transfers between devices  10.1 us (22%)
  Pallas kernels  6.52 us (14%)
  other arithmetic  0.81 us (2%)
  between operations  0.81 us (2%)
    ppermute x9, starting transfers between devices, sent_along(): lax.ppermute(value, ('band', 'group'), [(s[0] * MEMBERS + s[1], t[0] * ME...  28 us
    ppermute x9, waiting for transfers between devices, sent_along(): lax.ppermute(value, ('band', 'group'), [(s[0] * MEMBERS + s[1], t[0] * ME...  10.1 us
    pallas_call x1, Pallas kernels, shards(): call(functools.partial(own_kernel, count), planes, sources, OWN_SCRATCH)  3.55 us
    pallas_call x1, Pallas kernels, shards(): call(functools.partial(cross_kernel, count), slabs, [VMEM] * 5, PAIR_SCRA...  1.69 us
    pallas_call x1, Pallas kernels, shards(): packed = packing(False)(labels, source)[0]  1.15 us
  transfers between devices with their start and end apart: 9, of which 2 were waited for; matrix products, arithmetic and copies ran while one was open for 0% of the time, Pallas kernels for 12%

profile of v7, /device:TPU:1, one launch (start us, length us, event | category | flops | bytes accessed | tf_op | source)
XLA Modules:
  0.0 46.2 jit_solution(7501967814766237819)
XLA Ops:
  0.7 1.1 %shard_map.57.refs_1_ = bf16[64,4224]{1,0:T(8,128)(2,1)S(1)} custom-call(s32[1]{0:T(128)S(6)} %copy.8.label, bf16[64,4096]{1,0:T(8,128)(2,1)} %bitcast.4), custom_call_target="tpu_custom_call" | custom-call | bytes 4194304 | tf_op jit(solution)/shard_map/pallas_call | solution.py:290
  1.8 1.3 %collective-permute-start.2 = (bf16[64,4224]{1,0:T(8,128)(2,1)S(1)}, bf16[64,4224]{1,0:T(8,128)(2,1)S(1)}, u32[]{:S(2)}, u32[]{:S(2)}) collective-permute-start(bf16[64,4224]{1,0:T(8,128)(2,1)S(1)} %shard_map.57.refs_1_), channel_id=1, source_target_pairs={{4,0},{5,1},{6,2},{7,3},{8,4},{9,5},{10,6},{11,7},{12,8},{13,9},{1... | collective-permute-start | bytes 1622024 | tf_op jit(solution)/shard_map/ppermute | solution.py:259
  3.1 3.5 %shard_map.58 = (f32[64,4096]{1,0:T(8,128)S(1)}, f32[1024,256]{1,0:T(8,128)S(1)}, bf16[64,4096]{1,0:T(8,128)(2,1)S(1)}, bf16[512,256]{1,0:T(8,128)(2,1)S(1)}) custom-call(bf16[64,4096]{1,0:T(8,128)(2,1)} %bitcast.6, bf16[64,4224]{1,0:T(8,128)(2,1)S(1)} %shard_map.57.refs_1_, s32[64,4096]{1,0:T(8,128)} %refs_2_.3, bf16[512,256]{1,0:T(8,128)(2,1)} %constant.2.clone.refs_3_), custom_call_target="tpu_custom_call" | custom-call | flops 201326592 | bytes 4194304 | tf_op jit(solution)/shard_map/pallas_call | solution.py:299
  6.7 15.1 %collective-permute-start = (bf16[64,4224]{1,0:T(8,128)(2,1)S(1)}, bf16[64,4224]{1,0:T(8,128)(2,1)S(1)}, u32[]{:S(2)}, u32[]{:S(2)}) collective-permute-start(bf16[64,4224]{1,0:T(8,128)(2,1)S(1)} %shard_map.57.refs_1_), channel_id=1, source_target_pairs={{0,766},{1,767},{2,764},{3,765}} | collective-permute-start | bytes 1622024 | tf_op jit(solution)/shard_map/ppermute | solution.py:259
  21.7 0.1 shard_map.55.refs_1_
  21.8 0.7 %collective-permute-start.1 = (bf16[64,4224]{1,0:T(8,128)(2,1)S(1)}, bf16[64,4224]{1,0:T(8,128)(2,1)S(1)}, u32[]{:S(2)}, u32[]{:S(2)}) collective-permute-start(bf16[64,4224]{1,0:T(8,128)(2,1)S(1)} %shard_map.55.refs_1_), channel_id=1, source_target_pairs={{764,760},{765,761},{766,762},{767,763}} | collective-permute-start | bytes 1622024 | tf_op jit(solution)/shard_map/ppermute | solution.py:259
  22.5 0.1 shard_map.56
  22.6 0.0 collective-permute-done.2.packed
  22.6 1.7 %shard_map.59 = (f32[16,4096]{1,0:T(8,128)S(1)}, bf16[16,4096]{1,0:T(8,128)(2,1)S(1)}, bf16[16,4096]{1,0:T(8,128)(2,1)S(1)}, bf16[16,4096]{1,0:T(8,128)(2,1)S(1)}) custom-call(bf16[64,4096]{1,0:T(8,128)(2,1)S(1)} %get-tuple-element.29.target, bf16[64,4224]{1,0:T(8,128)(2,1)S(1)} %collective-permute-done.2.packed, f32[64,4096]{1,0:T(8,128)S(1)} %get-tuple-element.30.field, ...), custom_call_target="tpu_custom_call" | custom-call | flops 201326592 | bytes 4194304 | tf_op jit(solution)/shard_map/pallas_call | solution.py:310
  24.3 8.4 %collective-permute-done.from_first = bf16[64,4224]{1,0:T(8,128)(2,1)S(1)} collective-permute-done((bf16[64,4224]{1,0:T(8,128)(2,1)S(1)}, bf16[64,4224]{1,0:T(8,128)(2,1)S(1)}, u32[]{:S(2)}, u32[]{:S(2)}) %collective-permute-start) | collective-permute-done | bytes 540704 | tf_op jit(solution)/shard_map/ppermute | solution.py:259
  32.6 0.0 collective-permute-done.1.from_last
  32.7 0.7 %collective-permute-start.6 = (bf16[16,4096]{1,0:T(8,128)(2,1)S(1)}, bf16[16,4096]{1,0:T(8,128)(2,1)S(1)}, u32[]{:S(2)}, u32[]{:S(2)}) collective-permute-start(bf16[16,4096]{1,0:T(8,128)(2,1)S(1)} %get-tuple-element.38), channel_id=1, source_target_pairs={{760,762},{761,763},{762,760},{763,761},{764,766},{765,767},{766,7... | collective-permute-start | bytes 393224 | tf_op jit(solution)/shard_map/ppermute | solution.py:259
  33.4 0.7 %collective-permute-start.7 = (bf16[16,4096]{1,0:T(8,128)(2,1)S(1)}, bf16[16,4096]{1,0:T(8,128)(2,1)S(1)}, u32[]{:S(2)}, u32[]{:S(2)}) collective-permute-start(bf16[16,4096]{1,0:T(8,128)(2,1)S(1)} %get-tuple-element.39), channel_id=1, source_target_pairs={{760,763},{761,762},{762,761},{763,760},{764,767},{765,766},{766,7... | collective-permute-start | bytes 393224 | tf_op jit(solution)/shard_map/ppermute | solution.py:259
  34.0 0.7 %collective-permute-start.8 = (bf16[16,4096]{1,0:T(8,128)(2,1)S(1)}, bf16[16,4096]{1,0:T(8,128)(2,1)S(1)}, u32[]{:S(2)}, u32[]{:S(2)}) collective-permute-start(bf16[16,4096]{1,0:T(8,128)(2,1)S(1)} %get-tuple-element.40), channel_id=1, source_target_pairs={{760,761},{761,760},{762,763},{763,762},{764,765},{765,764},{766,7... | collective-permute-start | bytes 393224 | tf_op jit(solution)/shard_map/ppermute | solution.py:259
  34.7 1.9 %collective-permute-start.3 = (bf16[16,4096]{1,0:T(8,128)(2,1)S(1)}, bf16[16,4096]{1,0:T(8,128)(2,1)S(1)}, u32[]{:S(2)}, u32[]{:S(2)}) collective-permute-start(bf16[16,4096]{1,0:T(8,128)(2,1)S(1)} %get-tuple-element.35), channel_id=1, source_target_pairs={{0,2},{1,3},{2,0},{3,1},{4,6},{5,7},{6,4},{7,5},{8,10},{9,11},{10,... | collective-permute-start | bytes 393224 | tf_op jit(solution)/shard_map/ppermute | solution.py:259
  36.6 5.1 %collective-permute-start.4 = (bf16[16,4096]{1,0:T(8,128)(2,1)S(1)}, bf16[16,4096]{1,0:T(8,128)(2,1)S(1)}, u32[]{:S(2)}, u32[]{:S(2)}) collective-permute-start(bf16[16,4096]{1,0:T(8,128)(2,1)S(1)} %get-tuple-element.36), channel_id=1, source_target_pairs={{0,3},{1,2},{2,1},{3,0},{4,7},{5,6},{6,5},{7,4},{8,11},{9,10},{10,... | collective-permute-start | bytes 393224 | tf_op jit(solution)/shard_map/ppermute | solution.py:259
  41.7 0.0 collective-permute-done.6
  41.7 1.9 %collective-permute-start.5 = (bf16[16,4096]{1,0:T(8,128)(2,1)S(1)}, bf16[16,4096]{1,0:T(8,128)(2,1)S(1)}, u32[]{:S(2)}, u32[]{:S(2)}) collective-permute-start(bf16[16,4096]{1,0:T(8,128)(2,1)S(1)} %get-tuple-element.37), channel_id=1, source_target_pairs={{0,1},{1,0},{2,3},{3,2},{4,5},{5,4},{6,7},{7,6},{8,9},{9,8},{10,11... | collective-permute-start | bytes 393224 | tf_op jit(solution)/shard_map/ppermute | solution.py:259
  43.7 0.0 collective-permute-done.7
  43.7 0.0 collective-permute-done.8
  43.7 0.0 collective-permute-done.3
  43.7 1.7 %collective-permute-done.4 = bf16[16,4096]{1,0:T(8,128)(2,1)S(1)} collective-permute-done((bf16[16,4096]{1,0:T(8,128)(2,1)S(1)}, bf16[16,4096]{1,0:T(8,128)(2,1)S(1)}, u32[]{:S(2)}, u32[]{:S(2)}) %collective-permute-start.4) | collective-permute-done | bytes 131104 | tf_op jit(solution)/shard_map/ppermute | solution.py:259
  45.4 0.0 collective-permute-done.5
  45.4 0.8 %add_bitcast_fusion = f32[1,16,4096]{2,1,0:T(8,128)} fusion(bf16[16,4096]{1,0:T(8,128)(2,1)S(1)} %collective-permute-done.8, bf16[16,4096]{1,0:T(8,128)(2,1)S(1)} %collective-permute-done.7, bf16[16,4096]{1,0:T(8,128)(2,1)S(1)} %collective-permute-done.6, bf16[16,4096]{1,0:T(8,128)(2,1)S(1)} %collective-permute-done.5, ...), kind=kLoop, calls=%fused_computation | loop fusion | flops 786432 | bytes 1310720 | tf_op jit(solution)/shard_map/broadcast_in_dim | solution.py:319
  (1 shorter events, 0.0 us)
Async XLA Ops:
  1.8 20.8 %collective-permute-start.2 = (bf16[64,4224]{1,0:T(8,128)(2,1)S(1)}, bf16[64,4224]{1,0:T(8,128)(2,1)S(1)}, u32[]{:S(2)}, u32[]{:S(2)}) collective-permute-start(bf16[64,4224]{1,0:T(8,128)(2,1)S(1)} %shard_map.57.refs_1_), channel_id=1, source_target_pairs={{4,0},{5,1},{6,2},{7,3},{8,4},{9,5},{10,6},{11,7},{12,8},{13,9},{1... | collective-permute-start | bytes 1622024 | tf_op jit(solution)/shard_map/ppermute | solution.py:259
  6.7 26.0 %collective-permute-start = (bf16[64,4224]{1,0:T(8,128)(2,1)S(1)}, bf16[64,4224]{1,0:T(8,128)(2,1)S(1)}, u32[]{:S(2)}, u32[]{:S(2)}) collective-permute-start(bf16[64,4224]{1,0:T(8,128)(2,1)S(1)} %shard_map.57.refs_1_), channel_id=1, source_target_pairs={{0,766},{1,767},{2,764},{3,765}} | collective-permute-start | bytes 1622024 | tf_op jit(solution)/shard_map/ppermute | solution.py:259
  21.8 10.8 %collective-permute-start.1 = (bf16[64,4224]{1,0:T(8,128)(2,1)S(1)}, bf16[64,4224]{1,0:T(8,128)(2,1)S(1)}, u32[]{:S(2)}, u32[]{:S(2)}) collective-permute-start(bf16[64,4224]{1,0:T(8,128)(2,1)S(1)} %shard_map.55.refs_1_), channel_id=1, source_target_pairs={{764,760},{765,761},{766,762},{767,763}} | collective-permute-start | bytes 1622024 | tf_op jit(solution)/shard_map/ppermute | solution.py:259
  32.7 9.0 %collective-permute-start.6 = (bf16[16,4096]{1,0:T(8,128)(2,1)S(1)}, bf16[16,4096]{1,0:T(8,128)(2,1)S(1)}, u32[]{:S(2)}, u32[]{:S(2)}) collective-permute-start(bf16[16,4096]{1,0:T(8,128)(2,1)S(1)} %get-tuple-element.38), channel_id=1, source_target_pairs={{760,762},{761,763},{762,760},{763,761},{764,766},{765,767},{766,7... | collective-permute-start | bytes 393224 | tf_op jit(solution)/shard_map/ppermute | solution.py:259
  33.4 10.3 %collective-permute-start.7 = (bf16[16,4096]{1,0:T(8,128)(2,1)S(1)}, bf16[16,4096]{1,0:T(8,128)(2,1)S(1)}, u32[]{:S(2)}, u32[]{:S(2)}) collective-permute-start(bf16[16,4096]{1,0:T(8,128)(2,1)S(1)} %get-tuple-element.39), channel_id=1, source_target_pairs={{760,763},{761,762},{762,761},{763,760},{764,767},{765,766},{766,7... | collective-permute-start | bytes 393224 | tf_op jit(solution)/shard_map/ppermute | solution.py:259
  34.0 9.6 %collective-permute-start.8 = (bf16[16,4096]{1,0:T(8,128)(2,1)S(1)}, bf16[16,4096]{1,0:T(8,128)(2,1)S(1)}, u32[]{:S(2)}, u32[]{:S(2)}) collective-permute-start(bf16[16,4096]{1,0:T(8,128)(2,1)S(1)} %get-tuple-element.40), channel_id=1, source_target_pairs={{760,761},{761,760},{762,763},{763,762},{764,765},{765,764},{766,7... | collective-permute-start | bytes 393224 | tf_op jit(solution)/shard_map/ppermute | solution.py:259
  34.7 9.0 %collective-permute-start.3 = (bf16[16,4096]{1,0:T(8,128)(2,1)S(1)}, bf16[16,4096]{1,0:T(8,128)(2,1)S(1)}, u32[]{:S(2)}, u32[]{:S(2)}) collective-permute-start(bf16[16,4096]{1,0:T(8,128)(2,1)S(1)} %get-tuple-element.35), channel_id=1, source_target_pairs={{0,2},{1,3},{2,0},{3,1},{4,6},{5,7},{6,4},{7,5},{8,10},{9,11},{10,... | collective-permute-start | bytes 393224 | tf_op jit(solution)/shard_map/ppermute | solution.py:259
  36.6 8.7 %collective-permute-start.4 = (bf16[16,4096]{1,0:T(8,128)(2,1)S(1)}, bf16[16,4096]{1,0:T(8,128)(2,1)S(1)}, u32[]{:S(2)}, u32[]{:S(2)}) collective-permute-start(bf16[16,4096]{1,0:T(8,128)(2,1)S(1)} %get-tuple-element.36), channel_id=1, source_target_pairs={{0,3},{1,2},{2,1},{3,0},{4,7},{5,6},{6,5},{7,4},{8,11},{9,10},{10,... | collective-permute-start | bytes 393224 | tf_op jit(solution)/shard_map/ppermute | solution.py:259
  41.7 3.7 %collective-permute-start.5 = (bf16[16,4096]{1,0:T(8,128)(2,1)S(1)}, bf16[16,4096]{1,0:T(8,128)(2,1)S(1)}, u32[]{:S(2)}, u32[]{:S(2)}) collective-permute-start(bf16[16,4096]{1,0:T(8,128)(2,1)S(1)} %get-tuple-element.37), channel_id=1, source_target_pairs={{0,1},{1,0},{2,3},{3,2},{4,5},{5,4},{6,7},{7,6},{8,9},{9,8},{10,11... | collective-permute-start | bytes 393224 | tf_op jit(solution)/shard_map/ppermute | solution.py:259

commit v8 on v7

--- a/solution.py
+++ b/solution.py
@@ -64,8 +64,8 @@
 
 
 def gather_rows(column, turned, low):
-    first = turned[pl.ds(2 * column, HALF, stride=STRIDE), :]
-    second = turned[pl.ds(2 * column + 1, HALF, stride=STRIDE), :]
+    first = turned[pl.ds(2 * column, HALF, stride=STRIDE), :].astype(jnp.bfloat16)
+    second = turned[pl.ds(2 * column + 1, HALF, stride=STRIDE), :].astype(jnp.bfloat16)
     top, bottom = exchange(first, second, low)
     return jnp.concatenate([top, bottom], axis=0)
 
@@ -106,7 +106,7 @@
     for block in range(BLOCKS):
         back = jnp.concatenate(
             [gather_rows(2 * block + part, turned, low) for part in range(2)], axis=1
-        ).astype(jnp.bfloat16)
+        )
         potential = dot(h_cols, back)
         emit(block, potential * scale * by_owner(me, source, columns_of(block)).astype(jnp.float32))
 
@@ -266,7 +266,7 @@
 
 def exchanged(sent, bands):
     received = []
-    for bits in (2, 3, 1):
+    for bits in (3, 2, 1):
         pairs = [((b, g), (b, g ^ bits)) for b in bands for g in range(MEMBERS)]
         received.append(sent_along(sent[bits - 1], pairs))
     return received

time: 46.5 us -> 46.1 us (level)
  no operation moved by 1% of the time
where the time goes in v8:
time: 46.1 us; the launch traced here: 45.8 us
  starting transfers between devices  27.7 us (60%)
  waiting for transfers between devices  9.98 us (22%)
  Pallas kernels  6.51 us (14%)
  other arithmetic  0.81 us (2%)
  between operations  0.81 us (2%)
    ppermute x9, starting transfers between devices, sent_along(): lax.ppermute(value, ('band', 'group'), [(s[0] * MEMBERS + s[1], t[0] * ME...  27.7 us
    ppermute x9, waiting for transfers between devices, sent_along(): lax.ppermute(value, ('band', 'group'), [(s[0] * MEMBERS + s[1], t[0] * ME...  9.98 us
    pallas_call x1, Pallas kernels, shards(): call(functools.partial(own_kernel, count), planes, sources, OWN_SCRATCH)  3.55 us
    pallas_call x1, Pallas kernels, shards(): call(functools.partial(cross_kernel, count), slabs, [VMEM] * 5, PAIR_SCRA...  1.67 us
    pallas_call x1, Pallas kernels, shards(): packed = packing(False)(labels, source)[0]  1.15 us
  transfers between devices with their start and end apart: 9, of which 2 were waited for; matrix products, arithmetic and copies ran while one was open for 0% of the time, Pallas kernels for 12%

profile of v8, /device:TPU:1, one launch (start us, length us, event | category | flops | bytes accessed | tf_op | source)
XLA Modules:
  0.0 45.8 jit_solution(14607088823372763892)
XLA Ops:
  0.7 1.1 %shard_map.57.refs_1_ = bf16[64,4224]{1,0:T(8,128)(2,1)S(1)} custom-call(s32[1]{0:T(128)S(6)} %copy.8.label, bf16[64,4096]{1,0:T(8,128)(2,1)} %bitcast.4), custom_call_target="tpu_custom_call" | custom-call | bytes 4194304 | tf_op jit(solution)/shard_map/pallas_call | solution.py:290
  1.8 1.3 %collective-permute-start.2 = (bf16[64,4224]{1,0:T(8,128)(2,1)S(1)}, bf16[64,4224]{1,0:T(8,128)(2,1)S(1)}, u32[]{:S(2)}, u32[]{:S(2)}) collective-permute-start(bf16[64,4224]{1,0:T(8,128)(2,1)S(1)} %shard_map.57.refs_1_), channel_id=1, source_target_pairs={{4,0},{5,1},{6,2},{7,3},{8,4},{9,5},{10,6},{11,7},{12,8},{13,9},{1... | collective-permute-start | bytes 1622024 | tf_op jit(solution)/shard_map/ppermute | solution.py:259
  3.1 3.5 %shard_map.58 = (f32[64,4096]{1,0:T(8,128)S(1)}, f32[1024,256]{1,0:T(8,128)S(1)}, bf16[64,4096]{1,0:T(8,128)(2,1)S(1)}, bf16[512,256]{1,0:T(8,128)(2,1)S(1)}) custom-call(bf16[64,4096]{1,0:T(8,128)(2,1)} %bitcast.6, bf16[64,4224]{1,0:T(8,128)(2,1)S(1)} %shard_map.57.refs_1_, s32[64,4096]{1,0:T(8,128)} %refs_2_.3, bf16[512,256]{1,0:T(8,128)(2,1)} %constant.2.clone.refs_3_), custom_call_target="tpu_custom_call" | custom-call | flops 201326592 | bytes 4194304 | tf_op jit(solution)/shard_map/pallas_call | solution.py:299
  6.7 15.1 %collective-permute-start = (bf16[64,4224]{1,0:T(8,128)(2,1)S(1)}, bf16[64,4224]{1,0:T(8,128)(2,1)S(1)}, u32[]{:S(2)}, u32[]{:S(2)}) collective-permute-start(bf16[64,4224]{1,0:T(8,128)(2,1)S(1)} %shard_map.57.refs_1_), channel_id=1, source_target_pairs={{0,766},{1,767},{2,764},{3,765}} | collective-permute-start | bytes 1622024 | tf_op jit(solution)/shard_map/ppermute | solution.py:259
  21.7 0.1 shard_map.55.refs_1_
  21.8 0.7 %collective-permute-start.1 = (bf16[64,4224]{1,0:T(8,128)(2,1)S(1)}, bf16[64,4224]{1,0:T(8,128)(2,1)S(1)}, u32[]{:S(2)}, u32[]{:S(2)}) collective-permute-start(bf16[64,4224]{1,0:T(8,128)(2,1)S(1)} %shard_map.55.refs_1_), channel_id=1, source_target_pairs={{764,760},{765,761},{766,762},{767,763}} | collective-permute-start | bytes 1622024 | tf_op jit(solution)/shard_map/ppermute | solution.py:259
  22.5 0.1 shard_map.56
  22.6 0.0 collective-permute-done.2.packed
  22.6 1.7 %shard_map.59 = (f32[16,4096]{1,0:T(8,128)S(1)}, bf16[16,4096]{1,0:T(8,128)(2,1)S(1)}, bf16[16,4096]{1,0:T(8,128)(2,1)S(1)}, bf16[16,4096]{1,0:T(8,128)(2,1)S(1)}) custom-call(bf16[64,4096]{1,0:T(8,128)(2,1)S(1)} %get-tuple-element.29.target, bf16[64,4224]{1,0:T(8,128)(2,1)S(1)} %collective-permute-done.2.packed, f32[64,4096]{1,0:T(8,128)S(1)} %get-tuple-element.30.field, ...), custom_call_target="tpu_custom_call" | custom-call | flops 201326592 | bytes 4194304 | tf_op jit(solution)/shard_map/pallas_call | solution.py:310
  24.3 8.4 %collective-permute-done.from_first = bf16[64,4224]{1,0:T(8,128)(2,1)S(1)} collective-permute-done((bf16[64,4224]{1,0:T(8,128)(2,1)S(1)}, bf16[64,4224]{1,0:T(8,128)(2,1)S(1)}, u32[]{:S(2)}, u32[]{:S(2)}) %collective-permute-start) | collective-permute-done | bytes 540704 | tf_op jit(solution)/shard_map/ppermute | solution.py:259
  32.6 0.0 collective-permute-done.1.from_last
  32.7 0.7 %collective-permute-start.6 = (bf16[16,4096]{1,0:T(8,128)(2,1)S(1)}, bf16[16,4096]{1,0:T(8,128)(2,1)S(1)}, u32[]{:S(2)}, u32[]{:S(2)}) collective-permute-start(bf16[16,4096]{1,0:T(8,128)(2,1)S(1)} %get-tuple-element.38), channel_id=1, source_target_pairs={{760,763},{761,762},{762,761},{763,760},{764,767},{765,766},{766,7... | collective-permute-start | bytes 393224 | tf_op jit(solution)/shard_map/ppermute | solution.py:259
  33.4 0.7 %collective-permute-start.7 = (bf16[16,4096]{1,0:T(8,128)(2,1)S(1)}, bf16[16,4096]{1,0:T(8,128)(2,1)S(1)}, u32[]{:S(2)}, u32[]{:S(2)}) collective-permute-start(bf16[16,4096]{1,0:T(8,128)(2,1)S(1)} %get-tuple-element.39), channel_id=1, source_target_pairs={{760,762},{761,763},{762,760},{763,761},{764,766},{765,767},{766,7... | collective-permute-start | bytes 393224 | tf_op jit(solution)/shard_map/ppermute | solution.py:259
  34.0 0.7 %collective-permute-start.8 = (bf16[16,4096]{1,0:T(8,128)(2,1)S(1)}, bf16[16,4096]{1,0:T(8,128)(2,1)S(1)}, u32[]{:S(2)}, u32[]{:S(2)}) collective-permute-start(bf16[16,4096]{1,0:T(8,128)(2,1)S(1)} %get-tuple-element.40), channel_id=1, source_target_pairs={{760,761},{761,760},{762,763},{763,762},{764,765},{765,764},{766,7... | collective-permute-start | bytes 393224 | tf_op jit(solution)/shard_map/ppermute | solution.py:259
  34.7 3.3 %collective-permute-start.3 = (bf16[16,4096]{1,0:T(8,128)(2,1)S(1)}, bf16[16,4096]{1,0:T(8,128)(2,1)S(1)}, u32[]{:S(2)}, u32[]{:S(2)}) collective-permute-start(bf16[16,4096]{1,0:T(8,128)(2,1)S(1)} %get-tuple-element.35), channel_id=1, source_target_pairs={{0,3},{1,2},{2,1},{3,0},{4,7},{5,6},{6,5},{7,4},{8,11},{9,10},{10,... | collective-permute-start | bytes 393224 | tf_op jit(solution)/shard_map/ppermute | solution.py:259
  38.0 3.4 %collective-permute-start.4 = (bf16[16,4096]{1,0:T(8,128)(2,1)S(1)}, bf16[16,4096]{1,0:T(8,128)(2,1)S(1)}, u32[]{:S(2)}, u32[]{:S(2)}) collective-permute-start(bf16[16,4096]{1,0:T(8,128)(2,1)S(1)} %get-tuple-element.36), channel_id=1, source_target_pairs={{0,2},{1,3},{2,0},{3,1},{4,6},{5,7},{6,4},{7,5},{8,10},{9,11},{10,... | collective-permute-start | bytes 393224 | tf_op jit(solution)/shard_map/ppermute | solution.py:259
  41.4 0.0 collective-permute-done.6
  41.4 1.9 %collective-permute-start.5 = (bf16[16,4096]{1,0:T(8,128)(2,1)S(1)}, bf16[16,4096]{1,0:T(8,128)(2,1)S(1)}, u32[]{:S(2)}, u32[]{:S(2)}) collective-permute-start(bf16[16,4096]{1,0:T(8,128)(2,1)S(1)} %get-tuple-element.37), channel_id=1, source_target_pairs={{0,1},{1,0},{2,3},{3,2},{4,5},{5,4},{6,7},{7,6},{8,9},{9,8},{10,11... | collective-permute-start | bytes 393224 | tf_op jit(solution)/shard_map/ppermute | solution.py:259
  43.4 0.0 collective-permute-done.7
  43.4 0.0 collective-permute-done.8
  43.4 0.0 collective-permute-done.3
  43.4 1.6 %collective-permute-done.4 = bf16[16,4096]{1,0:T(8,128)(2,1)S(1)} collective-permute-done((bf16[16,4096]{1,0:T(8,128)(2,1)S(1)}, bf16[16,4096]{1,0:T(8,128)(2,1)S(1)}, u32[]{:S(2)}, u32[]{:S(2)}) %collective-permute-start.4) | collective-permute-done | bytes 131104 | tf_op jit(solution)/shard_map/ppermute | solution.py:259
  45.0 0.0 collective-permute-done.5
  45.0 0.8 %add_bitcast_fusion = f32[1,16,4096]{2,1,0:T(8,128)} fusion(bf16[16,4096]{1,0:T(8,128)(2,1)S(1)} %collective-permute-done.8, bf16[16,4096]{1,0:T(8,128)(2,1)S(1)} %collective-permute-done.7, bf16[16,4096]{1,0:T(8,128)(2,1)S(1)} %collective-permute-done.6, bf16[16,4096]{1,0:T(8,128)(2,1)S(1)} %collective-permute-done.5, ...), kind=kLoop, calls=%fused_computation | loop fusion | flops 786432 | bytes 1310720 | tf_op jit(solution)/shard_map/broadcast_in_dim | solution.py:319
  (1 shorter events, 0.0 us)
Async XLA Ops:
  1.8 20.8 %collective-permute-start.2 = (bf16[64,4224]{1,0:T(8,128)(2,1)S(1)}, bf16[64,4224]{1,0:T(8,128)(2,1)S(1)}, u32[]{:S(2)}, u32[]{:S(2)}) collective-permute-start(bf16[64,4224]{1,0:T(8,128)(2,1)S(1)} %shard_map.57.refs_1_), channel_id=1, source_target_pairs={{4,0},{5,1},{6,2},{7,3},{8,4},{9,5},{10,6},{11,7},{12,8},{13,9},{1... | collective-permute-start | bytes 1622024 | tf_op jit(solution)/shard_map/ppermute | solution.py:259
  6.7 26.0 %collective-permute-start = (bf16[64,4224]{1,0:T(8,128)(2,1)S(1)}, bf16[64,4224]{1,0:T(8,128)(2,1)S(1)}, u32[]{:S(2)}, u32[]{:S(2)}) collective-permute-start(bf16[64,4224]{1,0:T(8,128)(2,1)S(1)} %shard_map.57.refs_1_), channel_id=1, source_target_pairs={{0,766},{1,767},{2,764},{3,765}} | collective-permute-start | bytes 1622024 | tf_op jit(solution)/shard_map/ppermute | solution.py:259
  21.8 10.8 %collective-permute-start.1 = (bf16[64,4224]{1,0:T(8,128)(2,1)S(1)}, bf16[64,4224]{1,0:T(8,128)(2,1)S(1)}, u32[]{:S(2)}, u32[]{:S(2)}) collective-permute-start(bf16[64,4224]{1,0:T(8,128)(2,1)S(1)} %shard_map.55.refs_1_), channel_id=1, source_target_pairs={{764,760},{765,761},{766,762},{767,763}} | collective-permute-start | bytes 1622024 | tf_op jit(solution)/shard_map/ppermute | solution.py:259
  32.7 8.7 %collective-permute-start.6 = (bf16[16,4096]{1,0:T(8,128)(2,1)S(1)}, bf16[16,4096]{1,0:T(8,128)(2,1)S(1)}, u32[]{:S(2)}, u32[]{:S(2)}) collective-permute-start(bf16[16,4096]{1,0:T(8,128)(2,1)S(1)} %get-tuple-element.38), channel_id=1, source_target_pairs={{760,763},{761,762},{762,761},{763,760},{764,767},{765,766},{766,7... | collective-permute-start | bytes 393224 | tf_op jit(solution)/shard_map/ppermute | solution.py:259
  33.4 10.0 %collective-permute-start.7 = (bf16[16,4096]{1,0:T(8,128)(2,1)S(1)}, bf16[16,4096]{1,0:T(8,128)(2,1)S(1)}, u32[]{:S(2)}, u32[]{:S(2)}) collective-permute-start(bf16[16,4096]{1,0:T(8,128)(2,1)S(1)} %get-tuple-element.39), channel_id=1, source_target_pairs={{760,762},{761,763},{762,760},{763,761},{764,766},{765,767},{766,7... | collective-permute-start | bytes 393224 | tf_op jit(solution)/shard_map/ppermute | solution.py:259
  34.0 9.3 %collective-permute-start.8 = (bf16[16,4096]{1,0:T(8,128)(2,1)S(1)}, bf16[16,4096]{1,0:T(8,128)(2,1)S(1)}, u32[]{:S(2)}, u32[]{:S(2)}) collective-permute-start(bf16[16,4096]{1,0:T(8,128)(2,1)S(1)} %get-tuple-element.40), channel_id=1, source_target_pairs={{760,761},{761,760},{762,763},{763,762},{764,765},{765,764},{766,7... | collective-permute-start | bytes 393224 | tf_op jit(solution)/shard_map/ppermute | solution.py:259
  34.7 8.7 %collective-permute-start.3 = (bf16[16,4096]{1,0:T(8,128)(2,1)S(1)}, bf16[16,4096]{1,0:T(8,128)(2,1)S(1)}, u32[]{:S(2)}, u32[]{:S(2)}) collective-permute-start(bf16[16,4096]{1,0:T(8,128)(2,1)S(1)} %get-tuple-element.35), channel_id=1, source_target_pairs={{0,3},{1,2},{2,1},{3,0},{4,7},{5,6},{6,5},{7,4},{8,11},{9,10},{10,... | collective-permute-start | bytes 393224 | tf_op jit(solution)/shard_map/ppermute | solution.py:259
  38.0 7.0 %collective-permute-start.4 = (bf16[16,4096]{1,0:T(8,128)(2,1)S(1)}, bf16[16,4096]{1,0:T(8,128)(2,1)S(1)}, u32[]{:S(2)}, u32[]{:S(2)}) collective-permute-start(bf16[16,4096]{1,0:T(8,128)(2,1)S(1)} %get-tuple-element.36), channel_id=1, source_target_pairs={{0,2},{1,3},{2,0},{3,1},{4,6},{5,7},{6,4},{7,5},{8,10},{9,11},{10,... | collective-permute-start | bytes 393224 | tf_op jit(solution)/shard_map/ppermute | solution.py:259
  41.4 3.5 %collective-permute-start.5 = (bf16[16,4096]{1,0:T(8,128)(2,1)S(1)}, bf16[16,4096]{1,0:T(8,128)(2,1)S(1)}, u32[]{:S(2)}, u32[]{:S(2)}) collective-permute-start(bf16[16,4096]{1,0:T(8,128)(2,1)S(1)} %get-tuple-element.37), channel_id=1, source_target_pairs={{0,1},{1,0},{2,3},{3,2},{4,5},{5,4},{6,7},{7,6},{8,9},{9,8},{10,11... | collective-permute-start | bytes 393224 | tf_op jit(solution)/shard_map/ppermute | solution.py:259
